TPU v7x, 32 devices: a whole 2x2x4 slice. The times are simulated.
32 devices in a mesh: lon: 8 (over y, x, core), lat: 4 (over z).
Axes of the slice: x: 2, y: 2, z: 4, core: 2. Of those that a mesh axis runs over, the one named last changes fastest.
Arguments:
- latent: bfloat16 [4, 64, 128, 320], P(None, 'lat', 'lon'), may hold values from -28 to 28, as said below
- norm1_gain: float32 [320], replicated, may hold values from 0.1 to 1.9
- norm1_shift: float32 [320], replicated, may hold values from -3 to 3
- conv1_weight: bfloat16 [3, 3, 320, 320], replicated, may hold values from -0.109375 to 0.109375
- conv1_bias: float32 [320], replicated, may hold values from -3 to 3
- emb_shift: float32 [4, 320], replicated, may hold values from -4 to 4
- norm2_gain: float32 [320], replicated, may hold values from 0.1 to 1.9
- norm2_shift: float32 [320], replicated, may hold values from -3 to 3
- conv2_weight: bfloat16 [3, 3, 320, 320], replicated, may hold values from -0.109375 to 0.109375
- conv2_bias: float32 [320], replicated, may hold values from -3 to 3
Outputs:
- block_out: bfloat16 [4, 64, 128, 320], P(None, 'lat', 'lon')
Inputs may be any that keep to these rules, and one draw needn't show every extreme that they name: `latent`: Real-valued activations.
All inputs are finite; a program needn't handle non-finite values.
Results may differ from a plain program's by a relative error of at most 0.007.
Values may be sent and summed in bfloat16 or wider, within the bound.
No kernel may reach another device: no remote copies, remote signals or barrier semaphores. Data moves between devices by JAX's collectives and lax.ppermute only.
A program may use at most 64 MiB of HBM per device.

v0:
```python
import jax
import jax.numpy as jnp
from jax import lax
from jax.sharding import PartitionSpec as P

GROUPS = 32


def padded_2(array, sides, width, wrap):
    for axis, dim in sides:
        devices, length = (lax.axis_size(axis), array.shape[dim])
        up = [(i, (i + 1) % devices) for i in range(devices if wrap else devices - 1)]
        down = [(j, i) for i, j in up]
        last = lax.slice_in_dim(array, length - width, length, axis=dim)
        leading = lax.slice_in_dim(array, 0, width, axis=dim)
        before = lax.ppermute(last, axis, up)
        after = lax.ppermute(leading, axis, down)
        array = jnp.concatenate([before, array, after], axis=dim)
    return array


def from_behind(array, axis, by):
    devices = lax.axis_size(axis)
    return lax.ppermute(array, axis, [(i, (i + by) % devices) for i in range(devices)])


def group_stats(field, cell_count):
    frame_count = field.shape[0]
    grouped = field.reshape(frame_count, -1, GROUPS, field.shape[3] // GROUPS)
    summed, squares = lax.psum(
        (jnp.sum(grouped, axis=(1, 3)), jnp.sum(grouped * grouped, axis=(1, 3))), ("lon", "lat")
    )
    average = summed / cell_count
    variance = squares / cell_count - average * average
    return (average, lax.rsqrt(variance + 1e-05))


def activate(field, average, inverse, norm_gain, norm_shift):
    per_group = field.shape[3] // GROUPS
    per_mean = jnp.repeat(average, per_group, axis=1)[:, None, None, :]
    per_inverse = jnp.repeat(inverse, per_group, axis=1)[:, None, None, :]
    normed = (field - per_mean) * per_inverse * norm_gain + norm_shift
    return jax.nn.silu(normed).astype(jnp.bfloat16)


def sphere_pad(field):
    side_padded = padded_2(field, (("lon", 2),), 1, True)
    both_padded = padded_2(side_padded, (("lat", 1),), 1, False)
    north_row, south_row = from_behind(
        (side_padded[:, 0], side_padded[:, -1]), "lon", lax.axis_size("lon") // 2
    )
    lat_index = lax.axis_index("lat")
    first_row = jnp.where(lat_index == 0, north_row, both_padded[:, 0])
    final_row = jnp.where(lat_index == lax.axis_size("lat") - 1, south_row, both_padded[:, -1])
    return jnp.concatenate([first_row[:, None], both_padded[:, 1:-1], final_row[:, None]], axis=1)


def padded_input(source, cell_count, norm_gain, norm_shift):
    source_f = source.astype(jnp.float32)
    average, inverse = group_stats(source_f, cell_count)
    return sphere_pad(activate(source_f, average, inverse, norm_gain, norm_shift))


def convolve(padded, weight):
    return lax.conv_general_dilated(
        padded,
        weight,
        (1, 1),
        "VALID",
        dimension_numbers=("NHWC", "HWIO", "NHWC"),
        preferred_element_type=jnp.float32,
    )


def on_device(
    latent,
    norm1_gain,
    norm1_shift,
    conv1_weight,
    conv1_bias,
    emb_shift,
    norm2_gain,
    norm2_shift,
    conv2_weight,
    conv2_bias,
):
    per_group = latent.shape[3] // GROUPS
    cell_count = (
        latent.shape[1] * latent.shape[2] * lax.axis_size("lat") * lax.axis_size("lon") * per_group
    )
    first_padded = padded_input(latent, cell_count, norm1_gain, norm1_shift)
    hidden = convolve(first_padded, conv1_weight) + conv1_bias + emb_shift[:, None, None, :]
    hidden = hidden.astype(jnp.bfloat16)
    second_padded = padded_input(hidden, cell_count, norm2_gain, norm2_shift)
    branch = convolve(second_padded, conv2_weight) + conv2_bias
    return (latent.astype(jnp.float32) + branch).astype(jnp.bfloat16)


def solution(mesh):
    placed = (P(None, "lat", "lon", None), P(), P(), P(), P(), P(), P(), P(), P(), P())
    return jax.shard_map(
        on_device,
        mesh=mesh,
        in_specs=placed,
        out_specs=P(None, "lat", "lon", None),
        check_vma=False,
    )
```

profile of v0, /device:TPU:0, one launch (start us, length us, event | category | flops | bytes accessed | tf_op | source)
XLA Modules:
  0.0 154.9 jit_solution(12832509377845679093)
XLA Ops:
  0.0 2.1 %convert_reduce_fusion = (f32[4,320]{1,0:T(4,128)S(1)}, f32[4,320]{1,0:T(4,128)S(1)}) fusion(bf16[4,16,16,320]{3,2,1,0:T(8,128)(2,1)} %param.10), kind=kLoop, calls=%fused_computation.6 | loop fusion | flops 1308160 | bytes 665600 | tf_op jit(solution)/shard_map/reduce_sum | solution.py:31
  2.6 42.0 %all-reduce.1 = (f32[4,32]{1,0:T(4,128)S(1)}, f32[4,32]{1,0:T(4,128)S(1)}) all-reduce(f32[4,32]{1,0:T(4,128)S(1)} %reduce_sum.54, f32[4,32]{1,0:T(4,128)S(1)} %reduce_sum.51), channel_id=1, replica_groups=mesh['lon'=8,'lat'=4] {'lon','lat'}, use_global_device_ids=true, to_apply=%region_5.6 | all-reduce | flops 256 | bytes 2048 | tf_op jit(solution)/shard_map/psum | solution.py:30
  44.6 0.1 sub.26
  44.8 0.1 mul.59
  45.0 2.4 %fusion.18 = bf16[4,16,16,320]{3,0,2,1:T(4,128)(2,1)S(1)} fusion(f32[320]{0:T(512)} %param.12, f32[320]{0:T(512)} %param.11, f32[4,320]{1,0:T(4,128)S(1)} %mul.59, f32[4,320]{1,0:T(4,128)S(1)} %sub.26, bf16[4,16,16,320]{3,2,1,0:T(8,128)(2,1)} %param.10), kind=kLoop, calls=%fused_computation.32 | loop fusion | flops 3276800 | bytes 1323520 | tf_op jit(solution)/shard_map/convert_element_type | solution.py:43
  47.5 2.6 %collective-permute-start.1 = (bf16[4,16,1,320]{3,0,2,1:T(4,128)(2,1)S(1)}, bf16[4,16,1,320]{3,0,2,1:T(4,128)(2,1)S(1)}, u32[]{:S(2)}, u32[]{:S(2)}) collective-permute-start(bf16[4,16,1,320]{3,0,2,1:T(4,128)(2,1)S(1)} %get-tuple-element.18), channel_id=1, source_target_pairs={{4,0},{8,4},{12,8},{16,12},{20,16},{24,20},{28,24},{0,28},{5,1},{9... | collective-permute-start | bytes 122888 | tf_op jit(solution)/shard_map/ppermute | solution.py:17
  50.1 1.8 %collective-permute-done = bf16[4,16,1,320]{3,0,2,1:T(4,128)(2,1)S(1)} collective-permute-done((bf16[4,16,1,320]{3,0,2,1:T(4,128)(2,1)S(1)}, bf16[4,16,1,320]{3,0,2,1:T(4,128)(2,1)S(1)}, u32[]{:S(2)}, u32[]{:S(2)}) %collective-permute-start) | collective-permute-done | bytes 40992 | tf_op jit(solution)/shard_map/ppermute | solution.py:16
  52.0 2.3 %collective-permute-start.4 = (bf16[4,18,320]{2,0,1:T(4,128)(2,1)S(1)}, bf16[4,18,320]{2,0,1:T(4,128)(2,1)S(1)}, u32[]{:S(2)}, u32[]{:S(2)}) collective-permute-start(bf16[4,18,320]{2,0,1:T(4,128)(2,1)S(1)} %bitcast.78), channel_id=1, source_target_pairs={{0,16},{4,20},{8,24},{12,28},{16,0},{20,4},{24,8},{28,12},{1,17},{... | collective-permute-start | bytes 138248 | tf_op jit(solution)/shard_map/ppermute | solution.py:24
  54.3 1.3 collective-permute-start.5
  55.6 4.7 %collective-permute-start.3 = (bf16[4,1,18,320]{3,0,2,1:T(4,128)(2,1)S(1)}, bf16[4,1,18,320]{3,0,2,1:T(4,128)(2,1)S(1)}, u32[]{:S(2)}, u32[]{:S(2)}) collective-permute-start(bf16[4,1,18,320]{3,0,2,1:T(4,128)(2,1)S(1)} %get-tuple-element.14), channel_id=1, source_target_pairs={{0,1},{1,2},{2,3},{4,5},{5,6},{6,7},{8,9},{9,10},{10,11},{12,13},{... | collective-permute-start | bytes 138248 | tf_op jit(solution)/shard_map/ppermute | solution.py:16
  60.5 4.1 %collective-permute-done.2 = bf16[4,18,320]{2,0,1:T(4,128)(2,1)S(1)} collective-permute-done((bf16[4,18,320]{2,0,1:T(4,128)(2,1)S(1)}, bf16[4,18,320]{2,0,1:T(4,128)(2,1)S(1)}, u32[]{:S(2)}, u32[]{:S(2)}) %collective-permute-start.2) | collective-permute-done | bytes 46112 | tf_op jit(solution)/shard_map/ppermute | solution.py:24
  64.6 0.9 maximum_bitcast_fusion.1
  65.6 0.5 pad
  66.1 0.3 slice.44
  66.4 1.0 fusion.5
  67.5 0.2 broadcast.25
  67.6 0.5 copy-done.7
  68.1 7.1 %fusion.30 = (f32[16,32,3,320]{3,1,2,0:T(8,128)S(1)}, f32[16,32,3,320]{3,1,2,0:T(8,128)}) fusion(f32[16,32,3,320]{3,0,2,1:T(8,128)S(1)} %bitcast.75, f32[320]{0:T(512)S(1)} %copy-done.7, bf16[3,3,320,320]{3,2,1,0:T(8,128)(2,1)S(1)} %copy-done, bf16[18,4,8,5,320]{4,1,3,2,0:T(4,128)(2,1)S(1)} %fusion.5, pred[32,3]{0,1:T(4,128)(4,1)S(1)} %copy-done.9), kind=kOutput, calls=%fused_computation.59 | convolution fusion | flops 2834104320 | bytes 9586016 | tf_op jit(solution)/shard_map/conv_general_dilated | solution.py:65
  75.2 1.4 copy.121
  76.6 0.1 slice_reduce_fusion
  76.9 3.0 %copy.119 = f32[16,32,3,320]{3,0,2,1:T(8,128)S(1)} copy(f32[16,32,3,320]{3,1,2,0:T(8,128)} %get-tuple-element.24) | data formatting | bytes 3932160 | tf_op jit(solution)/shard_map/convert_element_type | solution.py:59
  80.2 39.4 %all-reduce = (f32[4,32]{1,0:T(4,128)S(1)}, f32[4,32]{1,0:T(4,128)S(1)}) all-reduce(f32[4,32]{1,0:T(4,128)S(1)} %reduce_sum.75, f32[4,32]{1,0:T(4,128)S(1)} %reduce_sum.72), channel_id=1, replica_groups=mesh['lon'=8,'lat'=4] {'lon','lat'}, use_global_device_ids=true, to_apply=%region_11.12 | all-reduce | flops 256 | bytes 2048 | tf_op jit(solution)/shard_map/psum | solution.py:30
  119.7 0.1 sub.30
  119.9 0.1 mul.67
  120.1 0.2 broadcast.27
  120.3 0.2 broadcast.26
  120.4 1.3 copy-done.1
  121.7 1.8 %multiply_convert_fusion = bf16[16,32,3,320]{3,1,2,0:T(8,128)(2,1)S(1)} fusion(f32[16,32,3,320]{3,0,2,1:T(8,128)S(1)} %bitcast.65, f32[16,32,3,320]{3,1,2,0:T(8,128)S(1)} %copy-done.1, f32[16,32,3,320]{3,0,2,1:T(8,128)S(1)} %bitcast.66, f32[320]{0:T(512)S(1)} %copy-done.4, f32[320]{0:T(512)S(1)} %copy-done.5), kind=kLoop, calls=%fused_computation.14 | loop fusion | flops 4423680 | bytes 6883840 | tf_op jit(solution)/shard_map/convert_element_type | solution.py:43
  123.5 0.4 copy.123
  124.1 2.6 %collective-permute-start.7 = (bf16[4,16,1,320]{3,1,2,0:T(8,128)(2,1)S(1)}, bf16[4,16,1,320]{3,1,2,0:T(8,128)(2,1)S(1)}, u32[]{:S(2)}, u32[]{:S(2)}) collective-permute-start(bf16[4,16,1,320]{3,1,2,0:T(8,128)(2,1)S(1)} %get-tuple-element.16), channel_id=1, source_target_pairs={{4,0},{8,4},{12,8},{16,12},{20,16},{24,20},{28,24},{0,28},{5,1},{9... | collective-permute-start | bytes 122888 | tf_op jit(solution)/shard_map/ppermute | solution.py:17
  126.7 1.8 %collective-permute-done.6 = bf16[4,16,1,320]{3,1,2,0:T(8,128)(2,1)S(1)} collective-permute-done((bf16[4,16,1,320]{3,1,2,0:T(8,128)(2,1)S(1)}, bf16[4,16,1,320]{3,1,2,0:T(8,128)(2,1)S(1)}, u32[]{:S(2)}, u32[]{:S(2)}) %collective-permute-start.6) | collective-permute-done | bytes 40992 | tf_op jit(solution)/shard_map/ppermute | solution.py:16
  128.5 0.2 pad_maximum_fusion.2
  128.7 2.3 %collective-permute-start.10 = (bf16[4,18,320]{2,0,1:T(4,128)(2,1)S(1)}, bf16[4,18,320]{2,0,1:T(4,128)(2,1)S(1)}, u32[]{:S(2)}, u32[]{:S(2)}) collective-permute-start(bf16[4,18,320]{2,0,1:T(4,128)(2,1)S(1)} %bitcast.77), channel_id=1, source_target_pairs={{0,16},{4,20},{8,24},{12,28},{16,0},{20,4},{24,8},{28,12},{1,17},{... | collective-permute-start | bytes 138248 | tf_op jit(solution)/shard_map/ppermute | solution.py:24
  131.1 1.3 collective-permute-start.11
  132.4 4.6 %collective-permute-start.9 = (bf16[4,1,18,320]{3,1,2,0:T(2,128)(2,1)S(1)}, bf16[4,1,18,320]{3,1,2,0:T(2,128)(2,1)S(1)}, u32[]{:S(2)}, u32[]{:S(2)}) collective-permute-start(bf16[4,1,18,320]{3,1,2,0:T(2,128)(2,1)S(1)} %get-tuple-element.12), channel_id=1, source_target_pairs={{0,1},{1,2},{2,3},{4,5},{5,6},{6,7},{8,9},{9,10},{10,11},{12,13},{... | collective-permute-start | bytes 138248 | tf_op jit(solution)/shard_map/ppermute | solution.py:16
  137.1 0.6 collective-permute-done.11
  137.9 3.3 %collective-permute-done.8 = bf16[4,18,320]{2,0,1:T(4,128)(2,1)S(1)} collective-permute-done((bf16[4,18,320]{2,0,1:T(4,128)(2,1)S(1)}, bf16[4,18,320]{2,0,1:T(4,128)(2,1)S(1)}, u32[]{:S(2)}, u32[]{:S(2)}) %collective-permute-start.8) | collective-permute-done | bytes 46112 | tf_op jit(solution)/shard_map/ppermute | solution.py:24
  141.3 0.9 maximum_bitcast_fusion
  142.2 0.4 copy.136
  142.6 0.5 pad.2.clone
  143.1 0.3 slice.50
  143.4 1.0 fusion.6
  144.5 0.5 copy-done.6
  145.0 5.0 %select_add_fusion = f32[16,32,3,320]{3,1,2,0:T(8,128)S(1)} fusion(bf16[3,3,320,320]{3,2,1,0:T(8,128)(2,1)S(1)} %copy-done.6, bf16[18,4,8,5,320]{4,1,3,2,0:T(4,128)(2,1)S(1)} %fusion.6, f32[320]{0:T(512)S(1)} %copy-done.8, pred[32,3]{0,1:T(4,128)(4,1)S(1)} %copy-done.9), kind=kOutput, calls=%fused_computation.13 | convolution fusion | flops 2832138240 | bytes 5653856 | tf_op jit(solution)/shard_map/conv_general_dilated | solution.py:65
  150.0 1.4 copy.132
  151.5 1.0 copy-done.2
  152.5 1.4 fusion.17
  154.0 1.0 copy.134
  (55 shorter events, 2.3 us)
Async XLA Ops:
  0.0 67.6 %copy-start = (bf16[3,3,320,320]{3,2,1,0:T(8,128)(2,1)S(1)}, bf16[3,3,320,320]{3,2,1,0:T(8,128)(2,1)}, u32[]{:S(2)}) copy-start(bf16[3,3,320,320]{3,2,1,0:T(8,128)(2,1)} %param.13) | copy-start | bytes 5529604
  47.4 4.5 %collective-permute-start = (bf16[4,16,1,320]{3,0,2,1:T(4,128)(2,1)S(1)}, bf16[4,16,1,320]{3,0,2,1:T(4,128)(2,1)S(1)}, u32[]{:S(2)}, u32[]{:S(2)}) collective-permute-start(bf16[4,16,1,320]{3,0,2,1:T(4,128)(2,1)S(1)} %get-tuple-element.17), channel_id=1, source_target_pairs={{0,4},{4,8},{8,12},{12,16},{16,20},{20,24},{24,28},{28,0},{1,5},{5... | collective-permute-start | bytes 122888 | tf_op jit(solution)/shard_map/ppermute | solution.py:16
  47.5 4.4 %collective-permute-start.1 = (bf16[4,16,1,320]{3,0,2,1:T(4,128)(2,1)S(1)}, bf16[4,16,1,320]{3,0,2,1:T(4,128)(2,1)S(1)}, u32[]{:S(2)}, u32[]{:S(2)}) collective-permute-start(bf16[4,16,1,320]{3,0,2,1:T(4,128)(2,1)S(1)} %get-tuple-element.18), channel_id=1, source_target_pairs={{4,0},{8,4},{12,8},{16,12},{20,16},{24,20},{28,24},{0,28},{5,1},{9... | collective-permute-start | bytes 122888 | tf_op jit(solution)/shard_map/ppermute | solution.py:17
  52.0 8.5 %collective-permute-start.4 = (bf16[4,18,320]{2,0,1:T(4,128)(2,1)S(1)}, bf16[4,18,320]{2,0,1:T(4,128)(2,1)S(1)}, u32[]{:S(2)}, u32[]{:S(2)}) collective-permute-start(bf16[4,18,320]{2,0,1:T(4,128)(2,1)S(1)} %bitcast.78), channel_id=1, source_target_pairs={{0,16},{4,20},{8,24},{12,28},{16,0},{20,4},{24,8},{28,12},{1,17},{... | collective-permute-start | bytes 138248 | tf_op jit(solution)/shard_map/ppermute | solution.py:24
  54.3 6.1 %collective-permute-start.5 = (bf16[4,1,18,320]{3,0,2,1:T(4,128)(2,1)S(1)}, bf16[4,1,18,320]{3,0,2,1:T(4,128)(2,1)S(1)}, u32[]{:S(2)}, u32[]{:S(2)}) collective-permute-start(bf16[4,1,18,320]{3,0,2,1:T(4,128)(2,1)S(1)} %get-tuple-element.13), channel_id=1, source_target_pairs={{1,0},{2,1},{3,2},{5,4},{6,5},{7,6},{9,8},{10,9},{11,10},{13,12},{... | collective-permute-start | bytes 138248 | tf_op jit(solution)/shard_map/ppermute | solution.py:17
  55.6 9.0 %collective-permute-start.3 = (bf16[4,1,18,320]{3,0,2,1:T(4,128)(2,1)S(1)}, bf16[4,1,18,320]{3,0,2,1:T(4,128)(2,1)S(1)}, u32[]{:S(2)}, u32[]{:S(2)}) collective-permute-start(bf16[4,1,18,320]{3,0,2,1:T(4,128)(2,1)S(1)} %get-tuple-element.14), channel_id=1, source_target_pairs={{0,1},{1,2},{2,3},{4,5},{5,6},{6,7},{8,9},{9,10},{10,11},{12,13},{... | collective-permute-start | bytes 138248 | tf_op jit(solution)/shard_map/ppermute | solution.py:16
  60.4 4.2 %collective-permute-start.2 = (bf16[4,18,320]{2,0,1:T(4,128)(2,1)S(1)}, bf16[4,18,320]{2,0,1:T(4,128)(2,1)S(1)}, u32[]{:S(2)}, u32[]{:S(2)}) collective-permute-start(bf16[4,18,320]{2,0,1:T(4,128)(2,1)S(1)} %bitcast.79), channel_id=1, source_target_pairs={{0,16},{4,20},{8,24},{12,28},{16,0},{20,4},{24,8},{28,12},{1,17},{... | collective-permute-start | bytes 138248 | tf_op jit(solution)/shard_map/ppermute | solution.py:24
  66.4 1.1 copy-start.3
  67.4 0.7 copy-start.7
  67.4 0.7 copy-start.9
  120.1 1.7 %copy-start.1 = (f32[16,32,3,320]{3,1,2,0:T(8,128)S(1)}, f32[16,32,3,320]{3,1,2,0:T(8,128)}, u32[]{:S(2)}) copy-start(f32[16,32,3,320]{3,1,2,0:T(8,128)} %get-tuple-element.24) | copy-start | bytes 5898244
  120.1 1.7 %copy-start.4 = (f32[320]{0:T(512)S(1)}, f32[320]{0:T(512)}, u32[]{:S(2)}) copy-start(f32[320]{0:T(512)} %param.17) | copy-start | bytes 3844
  120.1 1.7 %copy-start.5 = (f32[320]{0:T(512)S(1)}, f32[320]{0:T(512)}, u32[]{:S(2)}) copy-start(f32[320]{0:T(512)} %param.16) | copy-start | bytes 3844
  124.0 4.5 %collective-permute-start.6 = (bf16[4,16,1,320]{3,1,2,0:T(8,128)(2,1)S(1)}, bf16[4,16,1,320]{3,1,2,0:T(8,128)(2,1)S(1)}, u32[]{:S(2)}, u32[]{:S(2)}) collective-permute-start(bf16[4,16,1,320]{3,1,2,0:T(8,128)(2,1)S(1)} %get-tuple-element.15), channel_id=1, source_target_pairs={{0,4},{4,8},{8,12},{12,16},{16,20},{20,24},{24,28},{28,0},{1,5},{5... | collective-permute-start | bytes 122888 | tf_op jit(solution)/shard_map/ppermute | solution.py:16
  124.1 4.4 %collective-permute-start.7 = (bf16[4,16,1,320]{3,1,2,0:T(8,128)(2,1)S(1)}, bf16[4,16,1,320]{3,1,2,0:T(8,128)(2,1)S(1)}, u32[]{:S(2)}, u32[]{:S(2)}) collective-permute-start(bf16[4,16,1,320]{3,1,2,0:T(8,128)(2,1)S(1)} %get-tuple-element.16), channel_id=1, source_target_pairs={{4,0},{8,4},{12,8},{16,12},{20,16},{24,20},{28,24},{0,28},{5,1},{9... | collective-permute-start | bytes 122888 | tf_op jit(solution)/shard_map/ppermute | solution.py:17
  128.7 8.3 %collective-permute-start.10 = (bf16[4,18,320]{2,0,1:T(4,128)(2,1)S(1)}, bf16[4,18,320]{2,0,1:T(4,128)(2,1)S(1)}, u32[]{:S(2)}, u32[]{:S(2)}) collective-permute-start(bf16[4,18,320]{2,0,1:T(4,128)(2,1)S(1)} %bitcast.77), channel_id=1, source_target_pairs={{0,16},{4,20},{8,24},{12,28},{16,0},{20,4},{24,8},{28,12},{1,17},{... | collective-permute-start | bytes 138248 | tf_op jit(solution)/shard_map/ppermute | solution.py:24
  131.1 6.6 %collective-permute-start.11 = (bf16[4,1,18,320]{3,1,2,0:T(2,128)(2,1)S(1)}, bf16[4,1,18,320]{3,1,2,0:T(2,128)(2,1)S(1)}, u32[]{:S(2)}, u32[]{:S(2)}) collective-permute-start(bf16[4,1,18,320]{3,1,2,0:T(2,128)(2,1)S(1)} %get-tuple-element.11), channel_id=1, source_target_pairs={{1,0},{2,1},{3,2},{5,4},{6,5},{7,6},{9,8},{10,9},{11,10},{13,12},{... | collective-permute-start | bytes 138248 | tf_op jit(solution)/shard_map/ppermute | solution.py:17
  132.4 8.8 %collective-permute-start.9 = (bf16[4,1,18,320]{3,1,2,0:T(2,128)(2,1)S(1)}, bf16[4,1,18,320]{3,1,2,0:T(2,128)(2,1)S(1)}, u32[]{:S(2)}, u32[]{:S(2)}) collective-permute-start(bf16[4,1,18,320]{3,1,2,0:T(2,128)(2,1)S(1)} %get-tuple-element.12), channel_id=1, source_target_pairs={{0,1},{1,2},{2,3},{4,5},{5,6},{6,7},{8,9},{9,10},{10,11},{12,13},{... | collective-permute-start | bytes 138248 | tf_op jit(solution)/shard_map/ppermute | solution.py:16
  137.0 4.2 %collective-permute-start.8 = (bf16[4,18,320]{2,0,1:T(4,128)(2,1)S(1)}, bf16[4,18,320]{2,0,1:T(4,128)(2,1)S(1)}, u32[]{:S(2)}, u32[]{:S(2)}) collective-permute-start(bf16[4,18,320]{2,0,1:T(4,128)(2,1)S(1)} %bitcast.76), channel_id=1, source_target_pairs={{0,16},{4,20},{8,24},{12,28},{16,0},{20,4},{24,8},{28,12},{1,17},{... | collective-permute-start | bytes 138248 | tf_op jit(solution)/shard_map/ppermute | solution.py:24
  143.4 1.6 %copy-start.6 = (bf16[3,3,320,320]{3,2,1,0:T(8,128)(2,1)S(1)}, bf16[3,3,320,320]{3,2,1,0:T(8,128)(2,1)}, u32[]{:S(2)}) copy-start(bf16[3,3,320,320]{3,2,1,0:T(8,128)(2,1)} %param.18) | copy-start | bytes 5529604
  143.4 1.6 %copy-start.8 = (f32[320]{0:T(512)S(1)}, f32[320]{0:T(512)}, u32[]{:S(2)}) copy-start(f32[320]{0:T(512)} %param.19) | copy-start | bytes 3844
  151.4 1.1 copy-start.2
where the time goes:
time: 156 us; the launch traced here: 155 us
  blocking collectives  81.4 us (52%)
  starting transfers between devices  22.1 us (14%)
  local copies, waits for them, and re-layouts  14.6 us (9%)
  other arithmetic  12.7 us (8%)
  matrix products  12.1 us (8%)
  waiting for transfers between devices  11.6 us (7%)
    psum x2, blocking collectives, group_stats(): lax.psum((jnp.sum(grouped, axis=(1, 3)), jnp.sum(grouped * grouped, axis=...  81.4 us
    conv_general_dilated x2, matrix products, convolve(): lax.conv_general_dilated(padded, weight, (1, 1), 'VALID', dimension_numbe...  12.1 us
    ppermute x4, starting transfers between devices, padded_2(): before = lax.ppermute(last, axis, up)  9.4 us
    ppermute x4, starting transfers between devices, padded_2(): after = lax.ppermute(leading, axis, down)  7.82 us
    ppermute x4, waiting for transfers between devices, from_behind(): lax.ppermute(array, axis, [(i, (i + by) % devices) for i in range(devices)])  7.42 us
    ppermute x4, starting transfers between devices, from_behind(): lax.ppermute(array, axis, [(i, (i + by) % devices) for i in range(devices)])  4.85 us
    convert_element_type x2, other arithmetic, activate(): return jax.nn.silu(normed).astype(jnp.bfloat16)  4.24 us
    unnamed x21, local copies, waits for them, and re-layouts  3.76 us
  transfers between devices with their start and end apart: 12, of which 5 were waited for; matrix products, arithmetic and copies ran while one was open for 0% of the time, Pallas kernels for 0%

commit v1 on v0

v1 whole, which is shorter than its diff:
```python
import functools

import jax
import jax.numpy as jnp
from jax import lax
from jax.experimental import pallas as pl
from jax.experimental.pallas import tpu as pltpu
from jax.sharding import PartitionSpec as P

GROUPS = 32
EPS = 1e-05
AXES = ("lon", "lat")
F32 = jnp.float32
BF16 = jnp.bfloat16
EXACT = lax.Precision.HIGHEST
LANES = 128


def group_map(frames, channels):
    per_group = channels // GROUPS
    shape = (frames * GROUPS, channels)
    group = lax.rem(lax.broadcasted_iota(jnp.int32, shape, 0), GROUPS)
    channel = lax.broadcasted_iota(jnp.int32, shape, 1)
    low = group * per_group
    return ((channel >= low) & (channel < low + per_group)).astype(F32)


def own_lanes(frames):
    shape = (frames, frames * GROUPS)
    frame = lax.broadcasted_iota(jnp.int32, shape, 0) * GROUPS
    lane = lax.broadcasted_iota(jnp.int32, shape, 1)
    return (lane >= frame) & (lane < frame + GROUPS)


def pack(rows, groups, own):
    summed = lax.dot_general(rows, groups, (((1,), (1,)), ((), ())), precision=EXACT, preferred_element_type=F32)
    return jnp.sum(jnp.where(own, summed, 0.0), axis=0, keepdims=True)


def unpack(packed, groups, own):
    spread = jnp.where(own, jnp.broadcast_to(packed, own.shape), 0.0)
    return jnp.dot(spread, groups, precision=EXACT, preferred_element_type=F32)


def local_stats(load, frames, channels, cells, stats_ref):
    groups = group_map(frames, channels)
    own = own_lanes(frames)
    sums = jnp.concatenate(
        [jnp.sum(load(f), axis=0, keepdims=True) for f in range(frames)], axis=0
    )
    total = pack(sums, groups, own)
    mean = unpack(total * (1.0 / (cells * (channels // GROUPS))), groups, own)
    parts = []
    for f in range(frames):
        centred = load(f) - mean[f : f + 1]
        parts.append(jnp.sum(centred * centred, axis=0, keepdims=True))
    squares = pack(jnp.concatenate(parts, axis=0), groups, own)
    stats_ref[...] = jnp.broadcast_to(
        jnp.concatenate([total, squares], axis=0)[None], stats_ref.shape
    )


def merged_stats(stats_ref, local_count, frames, channels):
    groups = group_map(frames, channels)
    own = own_lanes(frames)
    stats = stats_ref[...]
    devices = stats.shape[0]
    sums, squares = stats[:, 0, :], stats[:, 1, :]
    mean = jnp.sum(sums, axis=0, keepdims=True) * (1.0 / (local_count * devices))
    apart = sums * (1.0 / local_count) - mean
    spread = jnp.sum(squares + local_count * (apart * apart), axis=0, keepdims=True)
    inverse = lax.rsqrt(spread * (1.0 / (local_count * devices)) + EPS)
    return unpack(mean, groups, own), unpack(inverse, groups, own)


def stats_kernel(x_ref, stats_ref):
    frames, height, width, channels = x_ref.shape

    def load(f):
        return x_ref[f].reshape(height * width, channels).astype(F32)

    local_stats(load, frames, channels, height * width, stats_ref)


def conv_kernel(
    last, flag_ref, x_ref, west_ref, east_ref, cw_ref, ccw_ref, stats_ref, gain_ref, shift_ref,
    weight_ref, bias_ref, *rest,
):
    if last:
        skip_ref, out_ref, act, taps, sem = rest
    else:
        out_ref, out_stats_ref, act, taps, sem = rest
    frames, height, width, channels = x_ref.shape
    main = (channels // 256) * 256
    tail = channels - main
    copies = []
    for dy in range(3):
        for dx in range(3):
            copies.append(pltpu.make_async_copy(
                weight_ref.at[dy, dx, 0:main], taps.at[dy, dx * main : (dx + 1) * main], sem.at[dy]))
            copies.append(pltpu.make_async_copy(
                weight_ref.at[dy, dx, main:channels],
                taps.at[dy, 3 * main + dx * tail : 3 * main + (dx + 1) * tail], sem.at[dy]))
    for copy in copies:
        copy.start()
    depth = 3 * channels
    if act.shape[3] > depth:
        act[:, :, :, depth:] = jnp.zeros(act.shape[:3] + (act.shape[3] - depth,), BF16)
        for dy in range(3):
            taps[dy, depth:] = jnp.zeros((taps.shape[1] - depth, channels), BF16)

    per_group = channels // GROUPS
    mean, inverse = merged_stats(stats_ref, float(height * width * per_group), frames, channels)
    scale = inverse * gain_ref[...]
    shift = shift_ref[...]
    first_is_north = flag_ref[0] == 1

    def put(f, row, dx, value):
        rows = value.shape[0]
        value = value.astype(BF16)
        act[f, row : row + rows, :, dx * main : (dx + 1) * main] = value[:, :, :main]
        at = 3 * main + dx * tail
        act[f, row : row + rows, :, at : at + tail] = value[:, :, main:]

    column = lax.broadcasted_iota(jnp.int32, (1, width, 1), 1)
    for f in range(frames):
        def activate(value):
            u = (value.astype(F32) - mean[f : f + 1]) * scale[f : f + 1] + shift
            return u / (1.0 + jnp.exp(-u))

        cw, ccw = activate(cw_ref[f]), activate(ccw_ref[f])
        north = jnp.where(first_is_north, cw, ccw)
        south = jnp.where(first_is_north, ccw, cw)
        west, east = activate(west_ref[f]), activate(east_ref[f])
        for dx in range(3):
            put(f, 0, dx, north[dx : dx + width][None])
            put(f, height + 1, dx, south[dx : dx + width][None])
        x = activate(x_ref[f].reshape(height * width, channels)).reshape(height, width, channels)
        put(f, 1, 1, x)
        left = jnp.where(column == 0, west[:, None, :], pltpu.roll(x, 1, 1))
        put(f, 1, 0, left)
        right = jnp.where(column == width - 1, east[:, None, :], pltpu.roll(x, width - 1, 1))
        put(f, 1, 2, right)

    total = None
    for dy in range(3):
        for copy in copies[6 * dy : 6 * dy + 6]:
            copy.wait()
        lhs = act[:, dy : dy + height].reshape(frames * height * width, act.shape[3])
        part = jnp.dot(lhs, taps[dy], preferred_element_type=F32)
        total = part if total is None else total + part

    cells = height * width
    for f in range(frames):
        value = total[f * cells : (f + 1) * cells] + bias_ref[f : f + 1]
        if last:
            value = value + skip_ref[f].reshape(cells, channels).astype(F32)
        out_ref[f] = value.astype(BF16).reshape(height, width, channels)
    if not last:
        def load(f):
            return out_ref[f].reshape(cells, channels).astype(F32)
        local_stats(load, frames, channels, cells, out_stats_ref)


VMEM = pl.BlockSpec(memory_space=pltpu.VMEM)
SMEM = pl.BlockSpec(memory_space=pltpu.SMEM)
ANY = pl.BlockSpec(memory_space=pl.ANY)


def call_stats(x, devices):
    frames = x.shape[0]
    return pl.pallas_call(
        stats_kernel,
        out_shape=jax.ShapeDtypeStruct((devices, 2, frames * GROUPS), F32),
        in_specs=[VMEM],
        out_specs=VMEM,
        name="first_stats",
    )(x)


def call_conv(flag, x, halo, stats, gain, shift, weight, bias, devices, skip=None):
    frames, height, width, channels = x.shape
    depth = -(-3 * channels // 256) * 256
    last = skip is not None
    out_shape = [jax.ShapeDtypeStruct(x.shape, BF16)]
    if not last:
        out_shape.append(jax.ShapeDtypeStruct((devices, 2, frames * GROUPS), F32))
    out = pl.pallas_call(
        functools.partial(conv_kernel, last),
        out_shape=out_shape,
        in_specs=[SMEM] + [VMEM] * 8 + [ANY] + [VMEM] * (2 if last else 1),
        out_specs=[VMEM] * len(out_shape),
        scratch_shapes=[
            pltpu.VMEM((frames, height + 2, width, depth), BF16),
            pltpu.VMEM((3, depth, channels), BF16),
            pltpu.SemaphoreType.DMA((3,)),
        ],
        name="second_conv" if last else "first_conv",
    )(flag, x, *halo, stats, gain[None], shift[None], weight, bias, *((skip,) if last else ()))
    return out[0] if last else out


def exchange_stats(stats):
    return lax.all_to_all(stats, AXES, 0, 0)


def halo_of(x):
    columns, rows = lax.axis_size("lon"), lax.axis_size("lat")
    half = columns // 2
    east_ring = [(k, (k + 1) % columns) for k in range(columns)]
    west_ring = [(b, a) for a, b in east_ring]
    clockwise = []
    for k in range(columns):
        for r in range(rows):
            if k < half:
                to = (k, r + 1) if r < rows - 1 else (k + half, r)
            else:
                to = (k, r - 1) if r > 0 else (k - half, r)
            clockwise.append((k * rows + r, to[0] * rows + to[1]))
    counter = [(b, a) for a, b in clockwise]
    west = lax.ppermute(x[:, :, -1], "lon", east_ring)
    east = lax.ppermute(x[:, :, 0], "lon", west_ring)

    def whole_row(i):
        return jnp.concatenate([west[:, i][:, None], x[:, i], east[:, i][:, None]], axis=1)

    downward = lax.axis_index("lon") < half
    first, final = whole_row(0), whole_row(-1)
    cw = lax.ppermute(jnp.where(downward, final, first), AXES, clockwise)
    ccw = lax.ppermute(jnp.where(downward, first, final), AXES, counter)
    return west, east, cw, ccw


def on_device(
    latent, norm1_gain, norm1_shift, conv1_weight, conv1_bias, emb_shift,
    norm2_gain, norm2_shift, conv2_weight, conv2_bias,
):
    devices = lax.axis_size("lon") * lax.axis_size("lat")
    frames, _, _, channels = latent.shape
    flag = (lax.axis_index("lon") < lax.axis_size("lon") // 2).astype(jnp.int32)[None]
    halo = halo_of(latent)
    stats = exchange_stats(call_stats(latent, devices))
    bias1 = conv1_bias[None] + emb_shift
    hidden, own = call_conv(flag, latent, halo, stats, norm1_gain, norm1_shift, conv1_weight, bias1, devices)
    halo = halo_of(hidden)
    stats = exchange_stats(own)
    bias2 = jnp.broadcast_to(conv2_bias[None], (frames, channels))
    return call_conv(flag, hidden, halo, stats, norm2_gain, norm2_shift, conv2_weight, bias2, devices, skip=latent)


def solution(mesh):
    placed = (P(None, "lat", "lon", None), P(), P(), P(), P(), P(), P(), P(), P(), P())
    return jax.shard_map(
        on_device,
        mesh=mesh,
        in_specs=placed,
        out_specs=P(None, "lat", "lon", None),
        check_vma=False,
    )
```

time: 156 us -> 63 us (0.40)
  blocking collectives: 81.4 us -> 0 us
  Pallas kernels: 0 us -> 21.7 us
  matrix products: 12.1 us -> 0 us
  other arithmetic: 12.7 us -> 1.46 us
  local copies, waits for them, and re-layouts: 14.6 us -> 9.29 us
  waiting for transfers between devices: 11.6 us -> 8.46 us
    psum x2 -> x0, blocking collectives: 81.4 us -> none  [group_stats(): lax.psum((jnp.sum(grouped, axis=(1, 3)), jnp.sum(grouped * grouped, axis=...]
    pallas_call x0 -> x3, Pallas kernels: none -> 21.7 us  [the longest x2 18.5 us: call_conv(): pl.pallas_call(functools.partial(conv_kernel, last), out_shape=out_shape,...]
    ppermute x12 -> x8, starting transfers between devices: 22.1 us -> 9.04 us  [the longest x2 4.19 us: halo_of(): east = lax.ppermute(x[:, :, 0], 'lon', west_ring)]
    all_to_all x0 -> x2, starting transfers between devices: none -> 12.2 us  [exchange_stats(): return lax.all_to_all(stats, AXES, 0, 0)]
    conv_general_dilated x2 -> x0, matrix products: 12.1 us -> none  [convolve(): lax.conv_general_dilated(padded, weight, (1, 1), 'VALID', dimension_numbe...]
    convert_element_type x3 -> x0, other arithmetic: 5.66 us -> none  [the longest x2 4.24 us: activate(): return jax.nn.silu(normed).astype(jnp.bfloat16)]
    convert_element_type x4 -> x0, local copies, waits for them, and re-layouts: 4.5 us -> none  [the longest x1 3.04 us: padded_input(): source_f = source.astype(jnp.float32)]
    broadcast_in_dim x6 -> x5, local copies, waits for them, and re-layouts: 0.47 us -> 4.29 us  [the longest x2 1.83 us: call_conv(): shift[None]]
  transfers between devices with their start and end apart: 12 -> 10, of which waited for: 5 -> 5; matrix products, arithmetic and copies ran while one was open for 0% -> 13% of each run, Pallas kernels for 0% -> 0%
where the time goes in v1:
time: 63 us; the launch traced here: 62.4 us
  Pallas kernels  21.7 us (34%)
  starting transfers between devices  21.2 us (34%)
  local copies, waits for them, and re-layouts  9.29 us (15%)
  waiting for transfers between devices  8.46 us (13%)
  other arithmetic  1.46 us (2%)
    pallas_call x2, Pallas kernels, call_conv(): pl.pallas_call(functools.partial(conv_kernel, last), out_shape=out_shape,...  18.5 us
    all_to_all x2, starting transfers between devices, exchange_stats(): return lax.all_to_all(stats, AXES, 0, 0)  12.2 us
    ppermute x2, waiting for transfers between devices, halo_of(): west = lax.ppermute(x[:, :, -1], 'lon', east_ring)  5.12 us
    ppermute x2, starting transfers between devices, halo_of(): east = lax.ppermute(x[:, :, 0], 'lon', west_ring)  4.19 us
    ppermute x2, starting transfers between devices, halo_of(): ccw = lax.ppermute(jnp.where(downward, first, final), AXES, counter)  3.65 us
    pallas_call x1, Pallas kernels, call_stats(): pl.pallas_call(stats_kernel, out_shape=jax.ShapeDtypeStruct((devices, 2,...  3.21 us
    ppermute x2, waiting for transfers between devices, halo_of(): cw = lax.ppermute(jnp.where(downward, final, first), AXES, clockwise)  2.25 us
    broadcast_in_dim x2, local copies, waits for them, and re-layouts, call_conv(): shift[None]  1.83 us
  transfers between devices with their start and end apart: 10, of which 5 were waited for; matrix products, arithmetic and copies ran while one was open for 13% of the time, Pallas kernels for 0%

profile of v1, /device:TPU:0, one launch (start us, length us, event | category | flops | bytes accessed | tf_op | source)
XLA Modules:
  0.0 62.4 jit_solution(16907620407991738112)
XLA Ops:
  0.0 3.2 %first_stats.1 = f32[32,2,128]{2,1,0:T(2,128)} custom-call(bf16[4,16,16,320]{3,2,1,0:T(8,128)(2,1)} %rest_0_.1), custom_call_target="tpu_custom_call" | custom-call | tf_op jit(solution)/shard_map/first_stats/pallas_call | solution.py:172
  3.2 7.3 %all-to-all-start = ((f32[32,2,128]{2,1,0:T(2,128)}), f32[32,2,128]{2,1,0:T(2,128)S(1)}, u32[]{:S(2)}, u32[]{:S(2)}) async-start(f32[32,2,128]{2,1,0:T(2,128)} %first_stats.1), calls=%async_computation | async-start | bytes 65536 | tf_op jit(solution)/shard_map/all_to_all | solution.py:204
  10.5 1.3 %fusion = (bf16[4,16,1,320]{3,2,1,0:T(2,128)(2,1)S(1)}, bf16[4,16,1,320]{3,2,1,0:T(2,128)(2,1)S(1)}) fusion(bf16[4,16,16,320]{3,2,1,0:T(8,128)(2,1)} %rest_0_.1), kind=kLoop, calls=%fused_computation.17 | loop fusion | bytes 163840 | tf_op jit(solution)/shard_map/slice | solution.py:222
  11.8 0.3 collective-permute-start
  12.2 2.4 %collective-permute-start.1 = (bf16[4,16,320]{2,1,0:T(8,128)(2,1)S(1)}, bf16[4,16,320]{2,1,0:T(8,128)(2,1)S(1)}, u32[]{:S(2)}, u32[]{:S(2)}) collective-permute-start(bf16[4,16,320]{2,1,0:T(8,128)(2,1)S(1)} %bitcast.24), channel_id=1, source_target_pairs={{4,0},{8,4},{12,8},{16,12},{20,16},{24,20},{28,24},{0,28},{5,1},{9... | collective-permute-start | bytes 122888 | tf_op jit(solution)/shard_map/ppermute | solution.py:222
  14.6 0.8 %slice_bitcast_fusion.5 = (bf16[4,16,320]{2,1,0:T(8,128)(2,1)S(1)}, bf16[4,16,320]{2,1,0:T(8,128)(2,1)S(1)}) fusion(bf16[4,16,16,320]{3,2,1,0:T(8,128)(2,1)} %rest_0_.1), kind=kLoop, calls=%fused_computation.15 | loop fusion | bytes 163840 | tf_op jit(solution)/shard_map/squeeze | solution.py:225
  15.4 0.9 %collective-permute-done.west_ref = bf16[4,16,320]{2,1,0:T(8,128)(2,1)S(1)} collective-permute-done((bf16[4,16,320]{2,1,0:T(8,128)(2,1)S(1)}, bf16[4,16,320]{2,1,0:T(8,128)(2,1)S(1)}, u32[]{:S(2)}, u32[]{:S(2)}) %collective-permute-start) | collective-permute-done | bytes 40992 | tf_op jit(solution)/shard_map/ppermute | solution.py:221
  16.4 0.0 collective-permute-done.1.east_ref
  16.4 0.0 copy-start.5
  16.4 0.1 broadcast_select_fusion.2
  16.5 1.8 %collective-permute-start.3 = (bf16[4,18,320]{2,1,0:T(8,128)(2,1)S(1)}, bf16[4,18,320]{2,1,0:T(8,128)(2,1)S(1)}, u32[]{:S(2)}, u32[]{:S(2)}) collective-permute-start(bf16[4,18,320]{2,1,0:T(8,128)(2,1)S(1)} %get-tuple-element.19), channel_id=1, source_target_pairs={{1,0},{2,1},{3,2},{19,3},{5,4},{6,5},{7,6},{23,7},{9,8},{10,9},{11... | collective-permute-start | bytes 138248 | tf_op jit(solution)/shard_map/ppermute | solution.py:230
  18.3 0.3 collective-permute-start.2
  18.6 1.3 %broadcast_add_fusion.bias_ref = f32[4,320]{1,0:T(4,128)} fusion(f32[4,320]{1,0:T(4,128)} %param.15, f32[320]{0:T(512)} %param.14), kind=kLoop, calls=%fused_computation.16 | loop fusion | flops 1280 | bytes 11520 | tf_op jit(solution)/shard_map/add | solution.py:243
  19.9 1.2 %broadcast_in_dim.26.gain_ref = f32[1,320]{1,0:T(1,128)} reshape(f32[320]{0:T(512)} %param.11) | data formatting | bytes 2560 | tf_op jit(solution)/shard_map/broadcast_in_dim | solution.py:199
  21.1 1.3 %broadcast_in_dim.27.shift_ref = f32[1,320]{1,0:T(1,128)} reshape(f32[320]{0:T(512)} %param.12) | data formatting | bytes 2560 | tf_op jit(solution)/shard_map/broadcast_in_dim | solution.py:199
  22.4 0.0 all-to-all-done.stats_ref
  22.4 0.0 collective-permute-done.3.ccw_ref
  22.4 0.0 copy-start.6
  22.4 0.4 collective-permute-done.2.cw_ref
  22.9 0.0 copy-done.4
  22.9 0.0 copy-done.5
  22.9 0.1 copy-done
  23.0 0.0 copy-done.6
  23.0 0.5 copy-done.7
  23.5 9.8 %first_conv.1 = (bf16[4,16,16,320]{3,2,1,0:T(8,128)(2,1)}, f32[32,2,128]{2,1,0:T(2,128)}) custom-call(s32[1]{0:T(128)} %bitcast.flag_ref, bf16[4,16,16,320]{3,2,1,0:T(8,128)(2,1)} %rest_0_.1, bf16[4,16,320]{2,1,0:T(8,128)(2,1)} %copy-done.4, bf16[4,16,320]{2,1,0:T(8,128)(2,1)} %copy-done.5, bf16[4,18,320]{2,1,0:T(8,128)(2,1)} %copy-done.7, ...), custom_call_target="tpu_custom_call" | custom-call | tf_op jit(solution)/shard_map/first_conv/pallas_call | solution.py:188
  33.4 1.3 %copy.15 = bf16[4,16,16,320]{3,1,0,2:T(8,128)(2,1)S(1)} copy(bf16[4,16,16,320]{3,2,1,0:T(8,128)(2,1)} %get-tuple-element.7.x_ref) | data formatting | bytes 1310720 | tf_op jit(solution)/shard_map/first_conv/pallas_call | solution.py:188
  34.7 1.7 %collective-permute-start.5 = (bf16[4,16,320]{2,1,0:T(8,128)(2,1)S(1)}, bf16[4,16,320]{2,1,0:T(8,128)(2,1)S(1)}, u32[]{:S(2)}, u32[]{:S(2)}) collective-permute-start(bf16[4,16,320]{2,1,0:T(8,128)(2,1)S(1)} %get-tuple-element.11), channel_id=1, source_target_pairs={{4,0},{8,4},{12,8},{16,12},{20,16},{24,20},{28,24},{0,28},{5,1},{9... | collective-permute-start | bytes 122888 | tf_op jit(solution)/shard_map/ppermute | solution.py:222
  36.4 0.8 %slice_bitcast_fusion.1 = (bf16[4,16,320]{2,1,0:T(8,128)(2,1)S(1)}, bf16[4,16,320]{2,1,0:T(8,128)(2,1)S(1)}) fusion(bf16[4,16,16,320]{3,2,1,0:T(8,128)(2,1)} %get-tuple-element.7.x_ref), kind=kLoop, calls=%fused_computation.9 | loop fusion | bytes 180224 | tf_op jit(solution)/shard_map/squeeze | solution.py:225
  37.3 4.8 %all-to-all-start.1 = ((f32[32,2,128]{2,1,0:T(2,128)}), f32[32,2,128]{2,1,0:T(2,128)S(1)}, u32[]{:S(2)}, u32[]{:S(2)}) async-start(f32[32,2,128]{2,1,0:T(2,128)} %get-tuple-element.8), calls=%async_computation.1 | async-start | bytes 65536 | tf_op jit(solution)/shard_map/all_to_all | solution.py:204
  42.1 0.3 collective-permute-start.4
  42.4 0.0 collective-permute-done.5.east_ref
  42.5 4.2 %collective-permute-done.4.west_ref = bf16[4,16,320]{2,1,0:T(8,128)(2,1)S(1)} collective-permute-done((bf16[4,16,320]{2,1,0:T(8,128)(2,1)S(1)}, bf16[4,16,320]{2,1,0:T(8,128)(2,1)S(1)}, u32[]{:S(2)}, u32[]{:S(2)}) %collective-permute-start.4) | collective-permute-done | bytes 40992 | tf_op jit(solution)/shard_map/ppermute | solution.py:221
  46.7 0.1 broadcast_select_fusion
  46.7 1.9 %collective-permute-start.7 = (bf16[4,18,320]{2,1,0:T(8,128)(2,1)S(1)}, bf16[4,18,320]{2,1,0:T(8,128)(2,1)S(1)}, u32[]{:S(2)}, u32[]{:S(2)}) collective-permute-start(bf16[4,18,320]{2,1,0:T(8,128)(2,1)S(1)} %get-tuple-element.17), channel_id=1, source_target_pairs={{1,0},{2,1},{3,2},{19,3},{5,4},{6,5},{7,6},{23,7},{9,8},{10,9},{11... | collective-permute-start | bytes 138248 | tf_op jit(solution)/shard_map/ppermute | solution.py:230
  48.6 0.3 collective-permute-start.6
  48.9 0.0 copy-done.10
  48.9 0.6 broadcast_in_dim.28.gain_ref
  49.5 0.0 copy-done.11
  49.5 0.6 broadcast_in_dim.29.shift_ref
  50.1 0.0 all-to-all-done.1.stats_ref
  50.1 1.1 %collective-permute-done.7.ccw_ref = bf16[4,18,320]{2,1,0:T(8,128)(2,1)S(1)} collective-permute-done((bf16[4,18,320]{2,1,0:T(8,128)(2,1)S(1)}, bf16[4,18,320]{2,1,0:T(8,128)(2,1)S(1)}, u32[]{:S(2)}, u32[]{:S(2)}) %collective-permute-start.7) | collective-permute-done | bytes 46112 | tf_op jit(solution)/shard_map/ppermute | solution.py:230
  51.2 1.8 %collective-permute-done.6.cw_ref = bf16[4,18,320]{2,1,0:T(8,128)(2,1)S(1)} collective-permute-done((bf16[4,18,320]{2,1,0:T(8,128)(2,1)S(1)}, bf16[4,18,320]{2,1,0:T(8,128)(2,1)S(1)}, u32[]{:S(2)}, u32[]{:S(2)}) %collective-permute-start.6) | collective-permute-done | bytes 46112 | tf_op jit(solution)/shard_map/ppermute | solution.py:229
  53.0 0.0 copy-done.12
  53.0 0.6 %broadcast_in_dim.30.bias_ref = f32[4,320]{1,0:T(4,128)} broadcast(f32[320]{0:T(512)S(1)} %copy-done.12), dimensions={1} | broadcast | bytes 6400 | tf_op jit(solution)/shard_map/broadcast_in_dim | solution.py:247
  53.6 0.0 copy-done.2
  53.6 0.0 copy-done.3
  53.6 0.0 copy-done.1
  53.6 8.6 %second_conv.1 = bf16[4,16,16,320]{3,2,1,0:T(8,128)(2,1)} custom-call(s32[1]{0:T(128)} %bitcast.flag_ref, bf16[4,16,16,320]{3,2,1,0:T(8,128)(2,1)} %get-tuple-element.7.x_ref, bf16[4,16,320]{2,1,0:T(8,128)(2,1)} %copy-done.3, bf16[4,16,320]{2,1,0:T(8,128)(2,1)} %copy-done.2, bf16[4,18,320]{2,1,0:T(8,128)(2,1)} %copy-done.9, bf16[4,18,320]{2,1,0:T(8,128)(2,1)} %copy-done.8, ...), custom_call_target="tpu_custom_call" | custom-call | tf_op jit(solution)/shard_map/second_conv/pallas_call | solution.py:188
  (20 shorter events, 0.1 us)
Async XLA Ops:
  3.2 19.2 %all-to-all-start = ((f32[32,2,128]{2,1,0:T(2,128)}), f32[32,2,128]{2,1,0:T(2,128)S(1)}, u32[]{:S(2)}, u32[]{:S(2)}) async-start(f32[32,2,128]{2,1,0:T(2,128)} %first_stats.1), calls=%async_computation | async-start | bytes 65536 | tf_op jit(solution)/shard_map/all_to_all | solution.py:204
  11.8 4.5 %collective-permute-start = (bf16[4,16,320]{2,1,0:T(8,128)(2,1)S(1)}, bf16[4,16,320]{2,1,0:T(8,128)(2,1)S(1)}, u32[]{:S(2)}, u32[]{:S(2)}) collective-permute-start(bf16[4,16,320]{2,1,0:T(8,128)(2,1)S(1)} %bitcast.23), channel_id=1, source_target_pairs={{0,4},{4,8},{8,12},{12,16},{16,20},{20,24},{24,28},{28,0},{1,5},{5... | collective-permute-start | bytes 122888 | tf_op jit(solution)/shard_map/ppermute | solution.py:221
  12.2 4.2 %collective-permute-start.1 = (bf16[4,16,320]{2,1,0:T(8,128)(2,1)S(1)}, bf16[4,16,320]{2,1,0:T(8,128)(2,1)S(1)}, u32[]{:S(2)}, u32[]{:S(2)}) collective-permute-start(bf16[4,16,320]{2,1,0:T(8,128)(2,1)S(1)} %bitcast.24), channel_id=1, source_target_pairs={{4,0},{8,4},{12,8},{16,12},{20,16},{24,20},{28,24},{0,28},{5,1},{9... | collective-permute-start | bytes 122888 | tf_op jit(solution)/shard_map/ppermute | solution.py:222
  16.4 6.5 %copy-start.4 = (bf16[4,16,320]{2,1,0:T(8,128)(2,1)}, bf16[4,16,320]{2,1,0:T(8,128)(2,1)S(1)}, u32[]{:S(2)}) copy-start(bf16[4,16,320]{2,1,0:T(8,128)(2,1)S(1)} %collective-permute-done.west_ref) | copy-start | bytes 122884
  16.4 6.5 %copy-start.5 = (bf16[4,16,320]{2,1,0:T(8,128)(2,1)}, bf16[4,16,320]{2,1,0:T(8,128)(2,1)S(1)}, u32[]{:S(2)}) copy-start(bf16[4,16,320]{2,1,0:T(8,128)(2,1)S(1)} %collective-permute-done.1.east_ref) | copy-start | bytes 122884
  16.5 5.9 %collective-permute-start.3 = (bf16[4,18,320]{2,1,0:T(8,128)(2,1)S(1)}, bf16[4,18,320]{2,1,0:T(8,128)(2,1)S(1)}, u32[]{:S(2)}, u32[]{:S(2)}) collective-permute-start(bf16[4,18,320]{2,1,0:T(8,128)(2,1)S(1)} %get-tuple-element.19), channel_id=1, source_target_pairs={{1,0},{2,1},{3,2},{19,3},{5,4},{6,5},{7,6},{23,7},{9,8},{10,9},{11... | collective-permute-start | bytes 138248 | tf_op jit(solution)/shard_map/ppermute | solution.py:230
  18.3 4.6 %collective-permute-start.2 = (bf16[4,18,320]{2,1,0:T(8,128)(2,1)S(1)}, bf16[4,18,320]{2,1,0:T(8,128)(2,1)S(1)}, u32[]{:S(2)}, u32[]{:S(2)}) collective-permute-start(bf16[4,18,320]{2,1,0:T(8,128)(2,1)S(1)} %get-tuple-element.20), channel_id=1, source_target_pairs={{0,1},{1,2},{2,3},{3,19},{4,5},{5,6},{6,7},{7,23},{8,9},{9,10},{10... | collective-permute-start | bytes 138248 | tf_op jit(solution)/shard_map/ppermute | solution.py:229
  22.4 0.6 copy-start
  22.4 0.6 %copy-start.6 = (bf16[4,18,320]{2,1,0:T(8,128)(2,1)}, bf16[4,18,320]{2,1,0:T(8,128)(2,1)S(1)}, u32[]{:S(2)}) copy-start(bf16[4,18,320]{2,1,0:T(8,128)(2,1)S(1)} %collective-permute-done.3.ccw_ref) | copy-start | bytes 138244
  22.9 0.6 %copy-start.7 = (bf16[4,18,320]{2,1,0:T(8,128)(2,1)}, bf16[4,18,320]{2,1,0:T(8,128)(2,1)S(1)}, u32[]{:S(2)}) copy-start(bf16[4,18,320]{2,1,0:T(8,128)(2,1)S(1)} %collective-permute-done.2.cw_ref) | copy-start | bytes 138244
  23.5 25.4 %copy-start.10 = (f32[320]{0:T(512)S(1)}, f32[320]{0:T(512)}, u32[]{:S(2)}) copy-start(f32[320]{0:T(512)} %param.16) | copy-start | bytes 3844
  23.5 26.0 %copy-start.11 = (f32[320]{0:T(512)S(1)}, f32[320]{0:T(512)}, u32[]{:S(2)}) copy-start(f32[320]{0:T(512)} %param.17) | copy-start | bytes 3844
  23.5 29.5 %copy-start.12 = (f32[320]{0:T(512)S(1)}, f32[320]{0:T(512)}, u32[]{:S(2)}) copy-start(f32[320]{0:T(512)} %param.19) | copy-start | bytes 3844
  34.7 7.7 %collective-permute-start.5 = (bf16[4,16,320]{2,1,0:T(8,128)(2,1)S(1)}, bf16[4,16,320]{2,1,0:T(8,128)(2,1)S(1)}, u32[]{:S(2)}, u32[]{:S(2)}) collective-permute-start(bf16[4,16,320]{2,1,0:T(8,128)(2,1)S(1)} %get-tuple-element.11), channel_id=1, source_target_pairs={{4,0},{8,4},{12,8},{16,12},{20,16},{24,20},{28,24},{0,28},{5,1},{9... | collective-permute-start | bytes 122888 | tf_op jit(solution)/shard_map/ppermute | solution.py:222
  37.3 12.8 %all-to-all-start.1 = ((f32[32,2,128]{2,1,0:T(2,128)}), f32[32,2,128]{2,1,0:T(2,128)S(1)}, u32[]{:S(2)}, u32[]{:S(2)}) async-start(f32[32,2,128]{2,1,0:T(2,128)} %get-tuple-element.8), calls=%async_computation.1 | async-start | bytes 65536 | tf_op jit(solution)/shard_map/all_to_all | solution.py:204
  42.1 4.5 %collective-permute-start.4 = (bf16[4,16,320]{2,1,0:T(8,128)(2,1)S(1)}, bf16[4,16,320]{2,1,0:T(8,128)(2,1)S(1)}, u32[]{:S(2)}, u32[]{:S(2)}) collective-permute-start(bf16[4,16,320]{2,1,0:T(8,128)(2,1)S(1)} %get-tuple-element.12), channel_id=1, source_target_pairs={{0,4},{4,8},{8,12},{12,16},{16,20},{20,24},{24,28},{28,0},{1,5},{5... | collective-permute-start | bytes 122888 | tf_op jit(solution)/shard_map/ppermute | solution.py:221
  42.4 11.2 %copy-start.2 = (bf16[4,16,320]{2,1,0:T(8,128)(2,1)}, bf16[4,16,320]{2,1,0:T(8,128)(2,1)S(1)}, u32[]{:S(2)}) copy-start(bf16[4,16,320]{2,1,0:T(8,128)(2,1)S(1)} %collective-permute-done.5.east_ref) | copy-start | bytes 122884
  46.6 7.0 %copy-start.3 = (bf16[4,16,320]{2,1,0:T(8,128)(2,1)}, bf16[4,16,320]{2,1,0:T(8,128)(2,1)S(1)}, u32[]{:S(2)}) copy-start(bf16[4,16,320]{2,1,0:T(8,128)(2,1)S(1)} %collective-permute-done.4.west_ref) | copy-start | bytes 122884
  46.7 4.4 %collective-permute-start.7 = (bf16[4,18,320]{2,1,0:T(8,128)(2,1)S(1)}, bf16[4,18,320]{2,1,0:T(8,128)(2,1)S(1)}, u32[]{:S(2)}, u32[]{:S(2)}) collective-permute-start(bf16[4,18,320]{2,1,0:T(8,128)(2,1)S(1)} %get-tuple-element.17), channel_id=1, source_target_pairs={{1,0},{2,1},{3,2},{19,3},{5,4},{6,5},{7,6},{23,7},{9,8},{10,9},{11... | collective-permute-start | bytes 138248 | tf_op jit(solution)/shard_map/ppermute | solution.py:230
  48.6 4.4 %collective-permute-start.6 = (bf16[4,18,320]{2,1,0:T(8,128)(2,1)S(1)}, bf16[4,18,320]{2,1,0:T(8,128)(2,1)S(1)}, u32[]{:S(2)}, u32[]{:S(2)}) collective-permute-start(bf16[4,18,320]{2,1,0:T(8,128)(2,1)S(1)} %get-tuple-element.18), channel_id=1, source_target_pairs={{0,1},{1,2},{2,3},{3,19},{4,5},{5,6},{6,7},{7,23},{8,9},{9,10},{10... | collective-permute-start | bytes 138248 | tf_op jit(solution)/shard_map/ppermute | solution.py:229
  50.1 3.5 %copy-start.1 = (f32[32,2,128]{2,1,0:T(2,128)}, f32[32,2,128]{2,1,0:T(2,128)S(1)}, u32[]{:S(2)}) copy-start(f32[32,2,128]{2,1,0:T(2,128)S(1)} %all-to-all-done.1.stats_ref) | copy-start | bytes 98308
  51.2 2.5 %copy-start.8 = (bf16[4,18,320]{2,1,0:T(8,128)(2,1)}, bf16[4,18,320]{2,1,0:T(8,128)(2,1)S(1)}, u32[]{:S(2)}) copy-start(bf16[4,18,320]{2,1,0:T(8,128)(2,1)S(1)} %collective-permute-done.7.ccw_ref) | copy-start | bytes 138244
  53.0 0.6 %copy-start.9 = (bf16[4,18,320]{2,1,0:T(8,128)(2,1)}, bf16[4,18,320]{2,1,0:T(8,128)(2,1)S(1)}, u32[]{:S(2)}) copy-start(bf16[4,18,320]{2,1,0:T(8,128)(2,1)S(1)} %collective-permute-done.6.cw_ref) | copy-start | bytes 138244

commit v2 on v1

v2 whole, which is shorter than its diff:
```python
import functools

import jax
import jax.numpy as jnp
from jax import lax
from jax.experimental import pallas as pl
from jax.experimental.pallas import tpu as pltpu
from jax.sharding import PartitionSpec as P


GROUPS = 32
EPS = 1e-05
AXES = ("lon", "lat")
F32 = jnp.float32
BF16 = jnp.bfloat16
LANES = 128
DEEP = 256
PARTS = 2
BEFORE = 3
VMEM = pl.BlockSpec(memory_space=pltpu.VMEM)
SMEM = pl.BlockSpec(memory_space=pltpu.SMEM)
HBM = pl.BlockSpec(memory_space=pltpu.MemorySpace.HBM)


def in_hbm(x):
    return pltpu.with_memory_space_constraint(x, pltpu.MemorySpace.HBM)


def group_map(frames, channels):
    per_group = channels // GROUPS
    shape = (frames * GROUPS, channels)
    group = lax.rem(lax.broadcasted_iota(jnp.int32, shape, 0), GROUPS)
    channel = lax.broadcasted_iota(jnp.int32, shape, 1)
    low = group * per_group
    return jnp.where((channel >= low) & (channel < low + per_group), 1.0, 0.0).astype(BF16)


def own_lanes(frames):
    shape = (frames, frames * GROUPS)
    frame = lax.broadcasted_iota(jnp.int32, shape, 0) * GROUPS
    lane = lax.broadcasted_iota(jnp.int32, shape, 1)
    return (lane >= frame) & (lane < frame + GROUPS)


def times_map(rows, groups, contract):
    high = rows.astype(BF16)
    rest = rows - high.astype(F32)
    middle = rest.astype(BF16)
    low = (rest - middle.astype(F32)).astype(BF16)
    return sum(
        lax.dot_general(part, groups, (((1,), (contract,)), ((), ())), preferred_element_type=F32)
        for part in (high, middle, low)
    )


def pack(rows, groups, own):
    summed = times_map(rows, groups, 1)
    return jnp.sum(jnp.where(own, summed, 0.0), axis=0, keepdims=True)


def unpack(packed, groups, own):
    return times_map(jnp.where(own, jnp.broadcast_to(packed, own.shape), 0.0), groups, 0)


def frame_sum(x_ref, f, term):
    _, height, width, channels = x_ref.shape
    total = jnp.zeros((8, channels), F32)
    for row in range(height):
        value = term(x_ref[f, row].astype(F32))
        total = total + jnp.sum(value.reshape(width // 8, 8, channels), axis=0)
    return jnp.sum(total, axis=0, keepdims=True)


def stats_kernel(x_ref, stats_ref):
    frames, height, width, channels = x_ref.shape
    sums = jnp.concatenate([frame_sum(x_ref, f, lambda v: v) for f in range(frames)], axis=0)
    groups = group_map(frames, channels)
    own = own_lanes(frames)
    total = pack(sums, groups, own)
    mean = unpack(total * (1.0 / (height * width * (channels // GROUPS))), groups, own)
    parts = []
    for f in range(frames):
        def squared(value, f=f):
            centred = value - mean[f : f + 1]
            return centred * centred

        parts.append(frame_sum(x_ref, f, squared))
    squares = pack(jnp.concatenate(parts, axis=0), groups, own)
    both = jnp.concatenate([total, squares], axis=0)
    stats_ref[...] = jnp.broadcast_to(both[None], stats_ref.shape)


def merged_stats(stats_ref, local_count, frames, channels):
    groups = group_map(frames, channels)
    own = own_lanes(frames)
    devices = stats_ref.shape[0]
    sums, squares = stats_ref[:, 0, :], stats_ref[:, 1, :]
    mean = jnp.sum(sums, axis=0, keepdims=True) * (1.0 / (local_count * devices))
    apart = sums * (1.0 / local_count) - mean
    spread = jnp.sum(squares + local_count * (apart * apart), axis=0, keepdims=True)
    inverse = lax.rsqrt(spread * (1.0 / (local_count * devices)) + EPS)
    return unpack(mean, groups, own), unpack(inverse, groups, own)


def put_edges(flag_ref, f, value, sides_ref, ends_ref):
    down, even = flag_ref[0] == 1, flag_ref[1] == 1
    first, final = value[:, 0, :], value[:, -1, :]
    sides_ref[0, f] = jnp.where(even, final, first)
    sides_ref[1, f] = jnp.where(even, first, final)
    ends_ref[0, f] = jnp.where(down, value[-1], value[0])
    ends_ref[1, f] = jnp.where(down, value[0], value[-1])


def edges_kernel(flag_ref, x_ref, copy_ref, sides_ref, ends_ref, sem):
    frames = x_ref.shape[0]
    copies = [pltpu.make_async_copy(x_ref.at[f], copy_ref.at[f], sem.at[f]) for f in range(frames)]
    for copy in copies:
        copy.start()
    for f in range(frames):
        copies[f].wait()
        put_edges(flag_ref, f, copy_ref[f], sides_ref, ends_ref)


def conv_kernel(
    last, flag_ref, x_ref, a_ref, b_ref, cw_ref, ccw_ref, stats_ref, gain_ref, shift_ref, bias_ref, extra_ref,
    weight_ref, out_ref, *rest,
):
    if last:
        staged_ref, out_sem, *rest = rest
    else:
        sides_ref, ends_ref, *rest = rest
        staged_ref = out_ref
    taps, tail_taps, side_taps, sem, *rest = rest
    grids, acts = rest[:PARTS], rest[PARTS:]
    frames, height, width, channels = x_ref.shape
    main = (channels // DEEP) * DEEP
    tail = channels - main
    tall, wide = height + 2, width + 2
    deep = tail_taps.shape[1] * tail
    lane_tiles = [(t, min(LANES, channels - t)) for t in range(0, channels, LANES)]

    copies = []
    for dy in range(3):
        copies.append((
            pltpu.make_async_copy(weight_ref.at[dy, :, 0:main], taps.at[dy], sem.at[dy, 0]),
            pltpu.make_async_copy(weight_ref.at[dy, :, main:channels], tail_taps.at[dy, 0:3], sem.at[dy, 1]),
        ))
    for pair in copies:
        for copy in pair:
            copy.start()

    def wait(dy):
        for copy in copies[dy]:
            copy.wait()

    if deep > 3 * tail:
        for dy in range(3):
            tail_taps[dy, 3:] = jnp.zeros((tail_taps.shape[1] - 3, tail, channels), BF16)
        for act in acts:
            act[:, :, :, 3 * channels :] = jnp.zeros(act.shape[:3] + (deep - 3 * tail,), BF16)

    per_group = channels // GROUPS
    mean, inverse = merged_stats(stats_ref, float(height * width * per_group), frames, channels)
    scale = inverse * (0.5 * gain_ref[...].reshape(1, channels))
    shift = 0.5 * shift_ref[...].reshape(1, channels)
    down, even = flag_ref[0] == 1, flag_ref[1] == 1
    per_part = frames // PARTS

    def prepare(f):
        grid, act, at = grids[f // per_part], acts[f // per_part], f % per_part

        def activate(value):
            part = (value.astype(F32) - mean[f : f + 1]) * scale[f : f + 1] + shift
            return part + part * jnp.tanh(part)

        def spot(row, column):
            return (at * tall + row) * wide + column

        def store(start, count, value, stride=1):
            for t, (lane, size) in enumerate(lane_tiles):
                where = pl.ds(start, count) if stride == 1 else pl.ds(start, count, stride)
                grid[t, where, 0:size] = value[:, lane : lane + size]

        cw, ccw, a, b = cw_ref[f], ccw_ref[f], a_ref[f], b_ref[f]
        store(spot(0, 0), wide, activate(jnp.where(down, cw, ccw)))
        store(spot(height + 1, 0), wide, activate(jnp.where(down, ccw, cw)))
        store(spot(1, 0), height, activate(jnp.where(even, b, a)), wide)
        store(spot(1, width + 1), height, activate(jnp.where(even, a, b)), wide)
        for row in range(height):
            store(spot(row + 1, 1), width, activate(x_ref[f, row]))
        for row in range(tall):
            for dx in range(3):
                for t, (lane, size) in enumerate(lane_tiles):
                    value = grid[t, pl.ds(spot(row, dx), width), 0:size].astype(BF16)
                    to = dx * main + lane if lane < main else 3 * main + dx * tail + lane - main
                    act[at, row, :, to : to + size] = value

    def tap(dy, low, high):
        above = taps[dy, :, :, low:high].reshape(3 * main, high - low)
        below = tail_taps[dy, :, :, low:high].reshape(deep, high - low)
        return jnp.concatenate([above, below], axis=0)

    def row_taps(part, dy):
        act = acts[part]
        lhs = act[:, dy : dy + height].reshape(per_part * height * width, act.shape[3])
        return jnp.dot(lhs, tap(dy, 0, main), preferred_element_type=F32)

    def side_of(part):
        act = acts[part]
        lhs = act[...].reshape(per_part * tall * width, act.shape[3])
        side = jnp.dot(lhs, side_taps[...], preferred_element_type=F32)
        side = side.reshape(per_part, tall, width, 3 * tail)
        return sum(side[:, dy : dy + height, :, dy * tail : (dy + 1) * tail] for dy in range(3))

    def finish(part, total, side):
        total = total.reshape(per_part, height, width, main)
        bias = bias_ref[...].reshape(1, 1, channels)
        for at in range(per_part):
            f = part * per_part + at
            for values, low, high in ((total, 0, main), (side, main, channels)):
                value = values[at] + bias[:, :, low:high]
                if last:
                    value = value + extra_ref[f, :, :, low:high].astype(F32)
                else:
                    value = value + extra_ref[f : f + 1, low:high].reshape(1, 1, high - low)
                staged_ref[f, :, :, low:high] = value.astype(BF16)
            if not last:
                put_edges(flag_ref, f, staged_ref[f], sides_ref, ends_ref)
        if last:
            span = pl.ds(part * per_part, per_part)
            pltpu.make_async_copy(staged_ref.at[span], out_ref.at[span], out_sem.at[part]).start()

    for f in range(BEFORE):
        prepare(f)
    for dy in range(3):
        wait(dy)
    for dy in range(3):
        side_taps[:, dy * tail : (dy + 1) * tail] = tap(dy, main, channels)
    for f in range(BEFORE, frames):
        prepare(f)
    for part in range(PARTS):
        finish(part, sum(row_taps(part, dy) for dy in range(3)), side_of(part))
    if last:
        for part in range(PARTS):
            span = pl.ds(part * per_part, per_part)
            pltpu.make_async_copy(staged_ref.at[span], out_ref.at[span], out_sem.at[part]).wait()


def edge_shapes(x):
    frames, height, width, channels = x.shape
    return [
        jax.ShapeDtypeStruct((2, frames, height, channels), BF16),
        jax.ShapeDtypeStruct((2, frames, width, channels), BF16),
    ]


def call_edges(flag, x):
    return pl.pallas_call(
        edges_kernel,
        out_shape=[jax.ShapeDtypeStruct(x.shape, x.dtype)] + edge_shapes(x),
        in_specs=[SMEM, HBM],
        out_specs=[VMEM] * 3,
        scratch_shapes=[pltpu.SemaphoreType.DMA((x.shape[0],))],
        name="edges",
        compiler_params=pltpu.CompilerParams(vmem_limit_bytes=8 << 20),
    )(flag, in_hbm(x))


def call_stats(x, devices):
    return pl.pallas_call(
        stats_kernel,
        out_shape=jax.ShapeDtypeStruct((devices, 2, x.shape[0] * GROUPS), F32),
        in_specs=[VMEM],
        out_specs=VMEM,
        name="own_stats",
        compiler_params=pltpu.CompilerParams(vmem_limit_bytes=8 << 20),
    )(x)


def call_conv(flag, x, halo, stats, gain, shift, weight, bias, extra, last):
    frames, height, width, channels = x.shape
    main = (channels // DEEP) * DEEP
    tail = channels - main
    slots = -(-3 * tail // DEEP) * DEEP // tail
    depth = 3 * main + slots * tail
    out_shape = [jax.ShapeDtypeStruct(x.shape, BF16)]
    cells = -(-(frames // PARTS) * (height + 2) * (width + 2) // 8) * 8
    scratch = [
        pltpu.VMEM((3, 3, main, channels), BF16),
        pltpu.VMEM((3, slots, tail, channels), BF16),
        pltpu.VMEM((depth, 3 * tail), BF16),
        pltpu.SemaphoreType.DMA((3, 2)),
    ]
    scratch += [pltpu.VMEM((-(-channels // LANES), cells, LANES), F32)] * PARTS
    scratch += [pltpu.VMEM((frames // PARTS, height + 2, width, depth), BF16)] * PARTS
    if last:
        out_specs = [HBM]
        scratch = [pltpu.VMEM(x.shape, BF16), pltpu.SemaphoreType.DMA((PARTS,))] + scratch
    else:
        out_shape += edge_shapes(x)
        out_specs = [VMEM] * 3
    out = pl.pallas_call(
        functools.partial(conv_kernel, last),
        out_shape=out_shape,
        in_specs=[SMEM] + [VMEM] * 10 + [HBM],
        out_specs=out_specs,
        scratch_shapes=scratch,
        name="second_conv" if last else "first_conv",
        compiler_params=pltpu.CompilerParams(vmem_limit_bytes=24 << 20),
    )(flag, x, *halo, stats, gain, shift, bias, extra, in_hbm(weight))
    return out[0] if last else out


def halo_of(sides, ends):
    columns, rows = lax.axis_size("lon"), lax.axis_size("lat")
    half = columns // 2
    down, even = lax.axis_index("lon") < half, lax.axis_index("lon") % 2 == 0
    paired = [(k, k ^ 1) for k in range(columns)]
    crossed = [(k, (k + 1) % columns if k % 2 else (k - 1) % columns) for k in range(columns)]
    clockwise = []
    for k in range(columns):
        for r in range(rows):
            if k < half:
                to = (k, r + 1) if r < rows - 1 else (k + half, r)
            else:
                to = (k, r - 1) if r > 0 else (k - half, r)
            clockwise.append((k * rows + r, to[0] * rows + to[1]))
    counter = [(b, a) for a, b in clockwise]
    a = lax.ppermute(sides[0], "lon", paired)
    b = lax.ppermute(sides[1], "lon", crossed)

    def whole_row(end, here):
        a_end = jnp.where(here, a[:, -1], a[:, 0])[:, None]
        b_end = jnp.where(here, b[:, -1], b[:, 0])[:, None]
        west, east = jnp.where(even, b_end, a_end), jnp.where(even, a_end, b_end)
        return jnp.concatenate([west, end, east], axis=1)

    cw = lax.ppermute(whole_row(ends[0], down), AXES, clockwise)
    ccw = lax.ppermute(whole_row(ends[1], ~down), AXES, counter)
    return a, b, cw, ccw


def gather_stats(x, devices):
    own = call_stats(x, devices)
    return lax.all_to_all(own, AXES, 0, 0)


def on_device(
    latent, norm1_gain, norm1_shift, conv1_weight, conv1_bias, emb_shift,
    norm2_gain, norm2_shift, conv2_weight, conv2_bias,
):
    devices = lax.axis_size("lon") * lax.axis_size("lat")
    column = lax.axis_index("lon")
    flag = jnp.stack([column < lax.axis_size("lon") // 2, column % 2 == 0]).astype(jnp.int32)
    latent, sides, ends = call_edges(flag, latent)
    halo = halo_of(sides, ends)
    stats = gather_stats(latent, devices)
    hidden, sides, ends = call_conv(
        flag, latent, halo, stats, norm1_gain, norm1_shift, conv1_weight, conv1_bias, emb_shift, False)
    halo = halo_of(sides, ends)
    stats = gather_stats(hidden, devices)
    return call_conv(
        flag, hidden, halo, stats, norm2_gain, norm2_shift, conv2_weight, conv2_bias, latent, True)


def solution(mesh):
    placed = (P(None, "lat", "lon", None), P(), P(), P(), P(), P(), P(), P(), P(), P())
    return jax.shard_map(
        on_device,
        mesh=mesh,
        in_specs=placed,
        out_specs=P(None, "lat", "lon", None),
        check_vma=False,
    )
```

time: 63 us -> 50.4 us (0.80)
  local copies, waits for them, and re-layouts: 9.29 us -> 0.08 us
  Pallas kernels: 21.7 us -> 16.2 us
  waiting for transfers between devices: 8.46 us -> 12.8 us
  other arithmetic: 1.46 us -> 0.3 us
    pallas_call x2, Pallas kernels: 18.5 us -> 10.7 us  [call_conv(): pl.pallas_call(functools.partial(conv_kernel, last), out_shape=out_shape,...]
    broadcast_in_dim x5 -> x0, local copies, waits for them, and re-layouts: 4.29 us -> none  [the longest x2 1.83 us: call_conv(): shift[None]]
    ppermute x8, waiting for transfers between devices: 8.46 us -> 12.1 us  [the longest x2 4.56 us: halo_of(): ccw = lax.ppermute(whole_row(ends[1], ~down), AXES, counter)]
    pallas_call x0 -> x1, Pallas kernels: none -> 1.86 us  [call_edges(): pl.pallas_call(edges_kernel, out_shape=[jax.ShapeDtypeStruct(x.shape, x.d...]
    squeeze x3 -> x4, local copies, waits for them, and re-layouts: 1.68 us -> 0.05 us  [the longest x2 0.02 us: halo_of(): b = lax.ppermute(sides[1], 'lon', crossed)]
    slice x5 -> x0, local copies, waits for them, and re-layouts: 1.33 us -> none  [the longest x1 1.27 us: halo_of(): east = lax.ppermute(x[:, :, 0], 'lon', west_ring)]
    pallas_call x1 -> x0, local copies, waits for them, and re-layouts: 1.31 us -> none  [call_conv(): pl.pallas_call(functools.partial(conv_kernel, last), out_shape=out_shape,...]
    add x1 -> x0, other arithmetic: 1.3 us -> none  [on_device(): bias1 = conv1_bias[None] + emb_shift]
  transfers between devices with their start and end apart: 10 -> 10, of which waited for: 5 -> 8; matrix products, arithmetic and copies ran while one was open for 13% -> 1% of each run, Pallas kernels for 0% -> 0%
where the time goes in v2:
time: 50.4 us; the launch traced here: 50.2 us
  starting transfers between devices  20.7 us (41%)
  Pallas kernels  16.2 us (32%)
  waiting for transfers between devices  12.8 us (25%)
    all_to_all x2, starting transfers between devices, gather_stats(): return lax.all_to_all(own, AXES, 0, 0)  11.2 us
    pallas_call x2, Pallas kernels, call_conv(): pl.pallas_call(functools.partial(conv_kernel, last), out_shape=out_shape,...  10.7 us
    ppermute x2, starting transfers between devices, halo_of(): b = lax.ppermute(sides[1], 'lon', crossed)  4.91 us
    ppermute x2, waiting for transfers between devices, halo_of(): ccw = lax.ppermute(whole_row(ends[1], ~down), AXES, counter)  4.56 us
    ppermute x2, starting transfers between devices, halo_of(): cw = lax.ppermute(whole_row(ends[0], down), AXES, clockwise)  4.44 us
    ppermute x2, waiting for transfers between devices, halo_of(): b = lax.ppermute(sides[1], 'lon', crossed)  4.11 us
    pallas_call x2, Pallas kernels, call_stats(): pl.pallas_call(stats_kernel, out_shape=jax.ShapeDtypeStruct((devices, 2,...  3.6 us
    ppermute x2, waiting for transfers between devices, halo_of(): cw = lax.ppermute(whole_row(ends[0], down), AXES, clockwise)  3.47 us
  transfers between devices with their start and end apart: 10, of which 8 were waited for; matrix products, arithmetic and copies ran while one was open for 1% of the time, Pallas kernels for 0%

profile of v2, /device:TPU:0, one launch (start us, length us, event | category | flops | bytes accessed | tf_op | source)
XLA Modules:
  0.0 50.2 jit_solution(9486049502598557194)
XLA Ops:
  0.0 0.0 copy-start
  0.0 0.0 copy-start.6
  0.0 0.0 copy-start.5
  0.0 0.0 copy-start.4
  0.0 0.1 add_convert_fusion.flag_ref
  0.1 1.9 %edges.1 = (bf16[4,16,16,320]{3,2,1,0:T(8,128)(2,1)S(1)}, bf16[2,4,16,320]{3,2,1,0:T(8,128)(2,1)S(1)}, bf16[2,4,16,320]{3,2,1,0:T(8,128)(2,1)S(1)}) custom-call(s32[2]{0:T(128)S(1)} %add_convert_fusion.flag_ref, bf16[4,16,16,320]{3,2,1,0:T(8,128)(2,1)} %x_ref.1), custom_call_target="tpu_custom_call" | custom-call | tf_op jit(solution)/shard_map/edges/pallas_call | solution.py:258
  2.0 1.8 %own_stats.2 = f32[32,2,128]{2,1,0:T(2,128)} custom-call(bf16[4,16,16,320]{3,2,1,0:T(8,128)(2,1)S(1)} %get-tuple-element.11.x_ref.extra_ref), custom_call_target="tpu_custom_call" | custom-call | tf_op jit(solution)/shard_map/own_stats/pallas_call | solution.py:270
  3.8 7.4 %all-to-all-start = ((f32[32,2,128]{2,1,0:T(2,128)}), f32[32,2,128]{2,1,0:T(2,128)S(1)}, u32[]{:S(2)}, u32[]{:S(2)}) async-start(f32[32,2,128]{2,1,0:T(2,128)} %own_stats.2), calls=%async_computation | async-start | bytes 65536 | tf_op jit(solution)/shard_map/all_to_all | solution.py:345
  11.1 2.5 %collective-permute-start.1 = (bf16[4,16,320]{2,1,0:T(8,128)(2,1)S(1)}, bf16[4,16,320]{2,1,0:T(8,128)(2,1)S(1)}, u32[]{:S(2)}, u32[]{:S(2)}) collective-permute-start(bf16[4,16,320]{2,1,0:T(8,128)(2,1)S(1)} %get-tuple-element.31), channel_id=1, source_target_pairs={{0,28},{4,8},{8,4},{12,16},{16,12},{20,24},{24,20},{28,0},{1,29},{... | collective-permute-start | bytes 122888 | tf_op jit(solution)/shard_map/ppermute | solution.py:330
  13.6 0.0 collective-permute-start
  13.6 2.1 %collective-permute-done.1.b_ref = bf16[4,16,320]{2,1,0:T(8,128)(2,1)S(1)} collective-permute-done((bf16[4,16,320]{2,1,0:T(8,128)(2,1)S(1)}, bf16[4,16,320]{2,1,0:T(8,128)(2,1)S(1)}, u32[]{:S(2)}, u32[]{:S(2)}) %collective-permute-start.1) | collective-permute-done | bytes 40992 | tf_op jit(solution)/shard_map/ppermute | solution.py:330
  15.7 0.0 collective-permute-done.a_ref
  15.8 2.2 %collective-permute-start.2 = (bf16[4,18,320]{2,1,0:T(8,128)(2,1)S(1)}, bf16[4,18,320]{2,1,0:T(8,128)(2,1)S(1)}, u32[]{:S(2)}, u32[]{:S(2)}) collective-permute-start(bf16[4,18,320]{2,1,0:T(8,128)(2,1)S(1)} %pad_maximum_fusion), channel_id=1, source_target_pairs={{0,1},{1,2},{2,3},{3,19},{4,5},{5,6},{6,7},{7,23},{8,9},{9,10},{10... | collective-permute-start | bytes 138248 | tf_op jit(solution)/shard_map/ppermute | solution.py:338
  18.0 0.0 copy-start.1
  18.0 0.0 copy-start.2
  18.0 0.0 copy-start.3
  18.1 0.1 collective-permute-start.3
  18.1 0.3 all-to-all-done.stats_ref
  18.4 1.7 %collective-permute-done.2.cw_ref = bf16[4,18,320]{2,1,0:T(8,128)(2,1)S(1)} collective-permute-done((bf16[4,18,320]{2,1,0:T(8,128)(2,1)S(1)}, bf16[4,18,320]{2,1,0:T(8,128)(2,1)S(1)}, u32[]{:S(2)}, u32[]{:S(2)}) %collective-permute-start.2) | collective-permute-done | bytes 46112 | tf_op jit(solution)/shard_map/ppermute | solution.py:338
  20.2 2.3 %collective-permute-done.3.ccw_ref = bf16[4,18,320]{2,1,0:T(8,128)(2,1)S(1)} collective-permute-done((bf16[4,18,320]{2,1,0:T(8,128)(2,1)S(1)}, bf16[4,18,320]{2,1,0:T(8,128)(2,1)S(1)}, u32[]{:S(2)}, u32[]{:S(2)}) %collective-permute-start.3) | collective-permute-done | bytes 46112 | tf_op jit(solution)/shard_map/ppermute | solution.py:339
  22.5 0.0 copy-done
  22.5 0.0 copy-done.6
  22.5 0.0 copy-done.5
  22.5 0.0 copy-done.4
  22.5 5.1 %first_conv.1 = (bf16[4,16,16,320]{3,2,1,0:T(8,128)(2,1)S(1)}, bf16[2,4,16,320]{3,2,1,0:T(8,128)(2,1)S(1)}, bf16[2,4,16,320]{3,2,1,0:T(8,128)(2,1)S(1)}) custom-call(s32[2]{0:T(128)S(1)} %add_convert_fusion.flag_ref, bf16[4,16,16,320]{3,2,1,0:T(8,128)(2,1)S(1)} %get-tuple-element.11.x_ref.extra_ref, bf16[4,16,320]{2,1,0:T(8,128)(2,1)S(1)} %collective-permute-done.a_ref, ...), custom_call_target="tpu_custom_call" | custom-call | tf_op jit(solution)/shard_map/first_conv/pallas_call | solution.py:302
  27.7 1.8 %own_stats.3 = f32[32,2,128]{2,1,0:T(2,128)} custom-call(bf16[4,16,16,320]{3,2,1,0:T(8,128)(2,1)S(1)} %get-tuple-element.14.x_ref), custom_call_target="tpu_custom_call" | custom-call | tf_op jit(solution)/shard_map/own_stats/pallas_call | solution.py:270
  29.5 3.8 %all-to-all-start.1 = ((f32[32,2,128]{2,1,0:T(2,128)}), f32[32,2,128]{2,1,0:T(2,128)S(1)}, u32[]{:S(2)}, u32[]{:S(2)}) async-start(f32[32,2,128]{2,1,0:T(2,128)} %own_stats.3), calls=%async_computation.1 | async-start | bytes 65536 | tf_op jit(solution)/shard_map/all_to_all | solution.py:345
  33.3 2.5 %collective-permute-start.5 = (bf16[4,16,320]{2,1,0:T(8,128)(2,1)S(1)}, bf16[4,16,320]{2,1,0:T(8,128)(2,1)S(1)}, u32[]{:S(2)}, u32[]{:S(2)}) collective-permute-start(bf16[4,16,320]{2,1,0:T(8,128)(2,1)S(1)} %get-tuple-element.23), channel_id=1, source_target_pairs={{0,28},{4,8},{8,4},{12,16},{16,12},{20,24},{24,20},{28,0},{1,29},{... | collective-permute-start | bytes 122888 | tf_op jit(solution)/shard_map/ppermute | solution.py:330
  35.8 0.0 collective-permute-start.4
  35.8 2.1 %collective-permute-done.5.b_ref = bf16[4,16,320]{2,1,0:T(8,128)(2,1)S(1)} collective-permute-done((bf16[4,16,320]{2,1,0:T(8,128)(2,1)S(1)}, bf16[4,16,320]{2,1,0:T(8,128)(2,1)S(1)}, u32[]{:S(2)}, u32[]{:S(2)}) %collective-permute-start.5) | collective-permute-done | bytes 40992 | tf_op jit(solution)/shard_map/ppermute | solution.py:330
  37.8 0.0 collective-permute-done.4.a_ref
  37.9 2.2 %collective-permute-start.6 = (bf16[4,18,320]{2,1,0:T(8,128)(2,1)S(1)}, bf16[4,18,320]{2,1,0:T(8,128)(2,1)S(1)}, u32[]{:S(2)}, u32[]{:S(2)}) collective-permute-start(bf16[4,18,320]{2,1,0:T(8,128)(2,1)S(1)} %pad_maximum_fusion.2), channel_id=1, source_target_pairs={{0,1},{1,2},{2,3},{3,19},{4,5},{5,6},{6,7},{7,23},{8,9},{9,10},{10... | collective-permute-start | bytes 138248 | tf_op jit(solution)/shard_map/ppermute | solution.py:338
  40.2 0.1 collective-permute-start.7
  40.2 0.4 all-to-all-done.1.stats_ref
  40.6 1.7 %collective-permute-done.6.cw_ref = bf16[4,18,320]{2,1,0:T(8,128)(2,1)S(1)} collective-permute-done((bf16[4,18,320]{2,1,0:T(8,128)(2,1)S(1)}, bf16[4,18,320]{2,1,0:T(8,128)(2,1)S(1)}, u32[]{:S(2)}, u32[]{:S(2)}) %collective-permute-start.6) | collective-permute-done | bytes 46112 | tf_op jit(solution)/shard_map/ppermute | solution.py:338
  42.3 2.3 %collective-permute-done.7.ccw_ref = bf16[4,18,320]{2,1,0:T(8,128)(2,1)S(1)} collective-permute-done((bf16[4,18,320]{2,1,0:T(8,128)(2,1)S(1)}, bf16[4,18,320]{2,1,0:T(8,128)(2,1)S(1)}, u32[]{:S(2)}, u32[]{:S(2)}) %collective-permute-start.7) | collective-permute-done | bytes 46112 | tf_op jit(solution)/shard_map/ppermute | solution.py:339
  44.6 0.0 copy-done.1
  44.6 0.0 copy-done.2
  44.6 0.0 copy-done.3
  44.6 5.6 %second_conv.1 = bf16[4,16,16,320]{3,2,1,0:T(8,128)(2,1)} custom-call(s32[2]{0:T(128)S(1)} %add_convert_fusion.flag_ref, bf16[4,16,16,320]{3,2,1,0:T(8,128)(2,1)S(1)} %get-tuple-element.14.x_ref, bf16[4,16,320]{2,1,0:T(8,128)(2,1)S(1)} %collective-permute-done.4.a_ref, bf16[4,16,320]{2,1,0:T(8,128)(2,1)S(1)} %collective-permute-done.5.b_ref, ...), custom_call_target="tpu_custom_call" | custom-call | tf_op jit(solution)/shard_map/second_conv/pallas_call | solution.py:302
  (10 shorter events, 0.3 us)
Async XLA Ops:
  0.0 22.5 %copy-start = (f32[4,320]{1,0:T(4,128)S(1)}, f32[4,320]{1,0:T(4,128)}, u32[]{:S(2)}) copy-start(f32[4,320]{1,0:T(4,128)} %extra_ref.1) | copy-start | bytes 15364
  0.0 22.5 %copy-start.6 = (f32[320]{0:T(512)S(1)}, f32[320]{0:T(512)}, u32[]{:S(2)}) copy-start(f32[320]{0:T(512)} %bias_ref.2) | copy-start | bytes 3844
  0.0 22.5 %copy-start.5 = (f32[320]{0:T(512)S(1)}, f32[320]{0:T(512)}, u32[]{:S(2)}) copy-start(f32[320]{0:T(512)} %shift_ref.2) | copy-start | bytes 3844
  0.0 22.5 %copy-start.4 = (f32[320]{0:T(512)S(1)}, f32[320]{0:T(512)}, u32[]{:S(2)}) copy-start(f32[320]{0:T(512)} %gain_ref.2) | copy-start | bytes 3844
  3.8 14.7 %all-to-all-start = ((f32[32,2,128]{2,1,0:T(2,128)}), f32[32,2,128]{2,1,0:T(2,128)S(1)}, u32[]{:S(2)}, u32[]{:S(2)}) async-start(f32[32,2,128]{2,1,0:T(2,128)} %own_stats.2), calls=%async_computation | async-start | bytes 65536 | tf_op jit(solution)/shard_map/all_to_all | solution.py:345
  11.1 4.5 %collective-permute-start.1 = (bf16[4,16,320]{2,1,0:T(8,128)(2,1)S(1)}, bf16[4,16,320]{2,1,0:T(8,128)(2,1)S(1)}, u32[]{:S(2)}, u32[]{:S(2)}) collective-permute-start(bf16[4,16,320]{2,1,0:T(8,128)(2,1)S(1)} %get-tuple-element.31), channel_id=1, source_target_pairs={{0,28},{4,8},{8,4},{12,16},{16,12},{20,24},{24,20},{28,0},{1,29},{... | collective-permute-start | bytes 122888 | tf_op jit(solution)/shard_map/ppermute | solution.py:330
  13.6 2.1 %collective-permute-start = (bf16[4,16,320]{2,1,0:T(8,128)(2,1)S(1)}, bf16[4,16,320]{2,1,0:T(8,128)(2,1)S(1)}, u32[]{:S(2)}, u32[]{:S(2)}) collective-permute-start(bf16[4,16,320]{2,1,0:T(8,128)(2,1)S(1)} %get-tuple-element.32), channel_id=1, source_target_pairs={{0,4},{4,0},{8,12},{12,8},{16,20},{20,16},{24,28},{28,24},{1,5},{5... | collective-permute-start | bytes 122888 | tf_op jit(solution)/shard_map/ppermute | solution.py:329
  15.8 4.4 %collective-permute-start.2 = (bf16[4,18,320]{2,1,0:T(8,128)(2,1)S(1)}, bf16[4,18,320]{2,1,0:T(8,128)(2,1)S(1)}, u32[]{:S(2)}, u32[]{:S(2)}) collective-permute-start(bf16[4,18,320]{2,1,0:T(8,128)(2,1)S(1)} %pad_maximum_fusion), channel_id=1, source_target_pairs={{0,1},{1,2},{2,3},{3,19},{4,5},{5,6},{6,7},{7,23},{8,9},{9,10},{10... | collective-permute-start | bytes 138248 | tf_op jit(solution)/shard_map/ppermute | solution.py:338
  18.0 26.6 %copy-start.1 = (f32[320]{0:T(512)S(1)}, f32[320]{0:T(512)}, u32[]{:S(2)}) copy-start(f32[320]{0:T(512)} %gain_ref.3) | copy-start | bytes 3844
  18.0 26.6 %copy-start.2 = (f32[320]{0:T(512)S(1)}, f32[320]{0:T(512)}, u32[]{:S(2)}) copy-start(f32[320]{0:T(512)} %shift_ref.3) | copy-start | bytes 3844
  18.0 26.5 %copy-start.3 = (f32[320]{0:T(512)S(1)}, f32[320]{0:T(512)}, u32[]{:S(2)}) copy-start(f32[320]{0:T(512)} %bias_ref.3) | copy-start | bytes 3844
  18.1 4.4 %collective-permute-start.3 = (bf16[4,18,320]{2,1,0:T(8,128)(2,1)S(1)}, bf16[4,18,320]{2,1,0:T(8,128)(2,1)S(1)}, u32[]{:S(2)}, u32[]{:S(2)}) collective-permute-start(bf16[4,18,320]{2,1,0:T(8,128)(2,1)S(1)} %pad_maximum_fusion.1), channel_id=1, source_target_pairs={{1,0},{2,1},{3,2},{19,3},{5,4},{6,5},{7,6},{23,7},{9,8},{10,9},{11... | collective-permute-start | bytes 138248 | tf_op jit(solution)/shard_map/ppermute | solution.py:339
  29.5 11.1 %all-to-all-start.1 = ((f32[32,2,128]{2,1,0:T(2,128)}), f32[32,2,128]{2,1,0:T(2,128)S(1)}, u32[]{:S(2)}, u32[]{:S(2)}) async-start(f32[32,2,128]{2,1,0:T(2,128)} %own_stats.3), calls=%async_computation.1 | async-start | bytes 65536 | tf_op jit(solution)/shard_map/all_to_all | solution.py:345
  33.3 4.5 %collective-permute-start.5 = (bf16[4,16,320]{2,1,0:T(8,128)(2,1)S(1)}, bf16[4,16,320]{2,1,0:T(8,128)(2,1)S(1)}, u32[]{:S(2)}, u32[]{:S(2)}) collective-permute-start(bf16[4,16,320]{2,1,0:T(8,128)(2,1)S(1)} %get-tuple-element.23), channel_id=1, source_target_pairs={{0,28},{4,8},{8,4},{12,16},{16,12},{20,24},{24,20},{28,0},{1,29},{... | collective-permute-start | bytes 122888 | tf_op jit(solution)/shard_map/ppermute | solution.py:330
  35.8 2.1 %collective-permute-start.4 = (bf16[4,16,320]{2,1,0:T(8,128)(2,1)S(1)}, bf16[4,16,320]{2,1,0:T(8,128)(2,1)S(1)}, u32[]{:S(2)}, u32[]{:S(2)}) collective-permute-start(bf16[4,16,320]{2,1,0:T(8,128)(2,1)S(1)} %get-tuple-element.24), channel_id=1, source_target_pairs={{0,4},{4,0},{8,12},{12,8},{16,20},{20,16},{24,28},{28,24},{1,5},{5... | collective-permute-start | bytes 122888 | tf_op jit(solution)/shard_map/ppermute | solution.py:329
  37.9 4.4 %collective-permute-start.6 = (bf16[4,18,320]{2,1,0:T(8,128)(2,1)S(1)}, bf16[4,18,320]{2,1,0:T(8,128)(2,1)S(1)}, u32[]{:S(2)}, u32[]{:S(2)}) collective-permute-start(bf16[4,18,320]{2,1,0:T(8,128)(2,1)S(1)} %pad_maximum_fusion.2), channel_id=1, source_target_pairs={{0,1},{1,2},{2,3},{3,19},{4,5},{5,6},{6,7},{7,23},{8,9},{9,10},{10... | collective-permute-start | bytes 138248 | tf_op jit(solution)/shard_map/ppermute | solution.py:338
  40.2 4.4 %collective-permute-start.7 = (bf16[4,18,320]{2,1,0:T(8,128)(2,1)S(1)}, bf16[4,18,320]{2,1,0:T(8,128)(2,1)S(1)}, u32[]{:S(2)}, u32[]{:S(2)}) collective-permute-start(bf16[4,18,320]{2,1,0:T(8,128)(2,1)S(1)} %pad_maximum_fusion.3), channel_id=1, source_target_pairs={{1,0},{2,1},{3,2},{19,3},{5,4},{6,5},{7,6},{23,7},{9,8},{10,9},{11... | collective-permute-start | bytes 138248 | tf_op jit(solution)/shard_map/ppermute | solution.py:339

commit v3 on v2

v3 whole, which is shorter than its diff:
```python
import functools

import jax
import jax.numpy as jnp
from jax import lax
from jax.experimental import pallas as pl
from jax.experimental.pallas import tpu as pltpu
from jax.sharding import PartitionSpec as P


GROUPS = 32
EPS = 1e-05
AXES = ("lon", "lat")
F32 = jnp.float32
BF16 = jnp.bfloat16
LANES = 128
DEEP = 256
PARTS = 2
VMEM = pl.BlockSpec(memory_space=pltpu.VMEM)
HBM = pl.BlockSpec(memory_space=pltpu.MemorySpace.HBM)


def in_hbm(x):
    return pltpu.with_memory_space_constraint(x, pltpu.MemorySpace.HBM)


def group_map(frames, channels):
    per_group = channels // GROUPS
    shape = (frames * GROUPS, channels)
    group = lax.rem(lax.broadcasted_iota(jnp.int32, shape, 0), GROUPS)
    channel = lax.broadcasted_iota(jnp.int32, shape, 1)
    low = group * per_group
    return jnp.where((channel >= low) & (channel < low + per_group), 1.0, 0.0).astype(BF16)


def own_lanes(frames):
    shape = (frames, frames * GROUPS)
    frame = lax.broadcasted_iota(jnp.int32, shape, 0) * GROUPS
    lane = lax.broadcasted_iota(jnp.int32, shape, 1)
    return (lane >= frame) & (lane < frame + GROUPS)


def times_map(rows, groups, contract):
    high = rows.astype(BF16)
    rest = rows - high.astype(F32)
    middle = rest.astype(BF16)
    low = (rest - middle.astype(F32)).astype(BF16)
    return sum(
        lax.dot_general(part, groups, (((1,), (contract,)), ((), ())), preferred_element_type=F32)
        for part in (high, middle, low)
    )


def pack(rows, groups, own):
    summed = times_map(rows, groups, 1)
    return jnp.sum(jnp.where(own, summed, 0.0), axis=0, keepdims=True)


def unpack(packed, groups, own):
    return times_map(jnp.where(own, jnp.broadcast_to(packed, own.shape), 0.0), groups, 0)


def frame_sum(x_ref, f, term):
    _, height, width, channels = x_ref.shape
    total = jnp.zeros((8, channels), F32)
    for row in range(height):
        value = term(x_ref[f, row].astype(F32))
        total = total + jnp.sum(value.reshape(width // 8, 8, channels), axis=0)
    return jnp.sum(total, axis=0, keepdims=True)


def frame_stats(x_ref, f):
    summed = frame_sum(x_ref, f, lambda value: value)
    mean = summed * (1.0 / (x_ref.shape[1] * x_ref.shape[2]))
    return summed, frame_sum(x_ref, f, lambda value: (value - mean) * (value - mean))


def write_stats(pairs, cells, stats_ref):
    sums = jnp.concatenate([p[0] for p in pairs], axis=0)
    squares = jnp.concatenate([p[1] for p in pairs], axis=0)
    frames, channels = sums.shape
    groups = group_map(frames, channels)
    own = own_lanes(frames)
    total = pack(sums, groups, own)
    mean = unpack(total * (1.0 / (cells * (channels // GROUPS))), groups, own)
    apart = sums * (1.0 / cells) - mean
    spread = pack(squares + cells * (apart * apart), groups, own)
    both = jnp.concatenate([total, spread], axis=0)
    stats_ref[...] = jnp.broadcast_to(both[None], stats_ref.shape)


def merged_stats(stats_ref, local_count, frames, channels):
    groups = group_map(frames, channels)
    own = own_lanes(frames)
    devices = stats_ref.shape[0]
    sums, squares = stats_ref[:, 0, :], stats_ref[:, 1, :]
    mean = jnp.sum(sums, axis=0, keepdims=True) * (1.0 / (local_count * devices))
    apart = sums * (1.0 / local_count) - mean
    spread = jnp.sum(squares + local_count * (apart * apart), axis=0, keepdims=True)
    inverse = lax.rsqrt(spread * (1.0 / (local_count * devices)) + EPS)
    return unpack(mean, groups, own), unpack(inverse, groups, own)


def place():
    column = lax.axis_index("lon")
    return column < lax.axis_size("lon") // 2, lax.rem(column, 2) == 0


def put_edges(f, value, sides_ref, ends_ref):
    down, even = place()
    first, final = value[:, 0, :], value[:, -1, :]
    sides_ref[0, f] = jnp.where(even, final, first)
    sides_ref[1, f] = jnp.where(even, first, final)
    ends_ref[0, f] = jnp.where(down, value[-1], value[0])
    ends_ref[1, f] = jnp.where(down, value[0], value[-1])


def tap_copies(weight_ref, dy, taps_ref, tails_ref, sem):
    main, tail = taps_ref.shape[1], tails_ref.shape[1]
    return (
        pltpu.make_async_copy(weight_ref.at[dy, :, 0:main], taps_ref, sem.at[0]),
        pltpu.make_async_copy(weight_ref.at[dy, :, main : main + tail], tails_ref.at[0:3], sem.at[1]),
    )


def clear_rest(tails_ref):
    if tails_ref.shape[0] > 3:
        tails_ref[3:] = jnp.zeros((tails_ref.shape[0] - 3,) + tails_ref.shape[1:], BF16)


def edges_kernel(
    x_ref, weight_ref, copy_ref, sides_ref, ends_ref, stats_ref, taps_ref, tails_ref, sem, tap_sem,
):
    frames, height, width, _ = x_ref.shape
    copies = [pltpu.make_async_copy(x_ref.at[f], copy_ref.at[f], sem.at[f]) for f in range(frames)]
    weights = tap_copies(weight_ref, 0, taps_ref, tails_ref, tap_sem)
    for copy in (*copies, *weights):
        copy.start()
    clear_rest(tails_ref)
    for copy in copies:
        copy.wait()
    pairs = []
    for f in range(frames):
        put_edges(f, copy_ref[f], sides_ref, ends_ref)
        pairs.append(frame_stats(copy_ref, f))
    write_stats(pairs, float(height * width), stats_ref)
    for copy in weights:
        copy.wait()


def conv_kernel(
    last, x_ref, a_ref, b_ref, cw_ref, ccw_ref, stats_ref, gain_ref, shift_ref, bias_ref,
    first_taps, first_tails, weight_ref, extra_ref, *rest,
):
    if last:
        out_ref, skip_ref, skip_sem, staged_ref, out_sem, *rest = rest
    else:
        next_ref, out_ref, sides_ref, ends_ref, own_stats_ref, next_taps, next_tails, next_sem, *rest = rest
        staged_ref = out_ref
    taps, tails, side_taps, sem, *rest = rest
    grids, acts, sums = rest[:PARTS], rest[PARTS : 2 * PARTS], rest[2 * PARTS :]
    frames, height, width, channels = x_ref.shape
    main = (channels // DEEP) * DEEP
    tail = channels - main
    tall, wide = height + 2, width + 2
    deep = tails.shape[1] * tail
    lane_tiles = [(t, min(LANES, channels - t)) for t in range(0, channels, LANES)]
    per_part = frames // PARTS

    copies = [
        copy for dy in (1, 2)
        for copy in tap_copies(weight_ref, dy, taps.at[dy - 1], tails.at[dy - 1], sem.at[dy - 1])
    ]
    for copy in copies:
        copy.start()
    if last:
        skip_copy = pltpu.make_async_copy(extra_ref, skip_ref, skip_sem.at[0])
        skip_copy.start()
    else:
        next_copies = tap_copies(next_ref, 0, next_taps, next_tails, next_sem)
        clear_rest(next_tails)
    for dy in (1, 2):
        clear_rest(tails.at[dy - 1])

    @pl.when(lax.axis_index("lon") >= 0)
    def _():
        if deep > 3 * tail:
            for act in acts:
                act[:, :, :, 3 * channels :] = jnp.zeros(act.shape[:3] + (deep - 3 * tail,), BF16)

        per_group = channels // GROUPS
        mean, inverse = merged_stats(stats_ref, float(height * width * per_group), frames, channels)
        scale = inverse * (0.5 * gain_ref[...].reshape(1, channels))
        shift = 0.5 * shift_ref[...].reshape(1, channels)
        down, even = place()

        def prepare(f):
            grid, act, at = grids[f // per_part], acts[f // per_part], f % per_part

            def activate(value):
                part = (value.astype(F32) - mean[f : f + 1]) * scale[f : f + 1] + shift
                return part + part * jnp.tanh(part)

            def spot(row, column):
                return (at * tall + row) * wide + column

            def store(start, count, value, stride=1):
                for t, (lane, size) in enumerate(lane_tiles):
                    where = pl.ds(start, count) if stride == 1 else pl.ds(start, count, stride)
                    grid[t, where, 0:size] = value[:, lane : lane + size]

            cw, ccw, a, b = cw_ref[f], ccw_ref[f], a_ref[f], b_ref[f]
            store(spot(0, 0), wide, activate(jnp.where(down, cw, ccw)))
            store(spot(height + 1, 0), wide, activate(jnp.where(down, ccw, cw)))
            store(spot(1, 0), height, activate(jnp.where(even, b, a)), wide)
            store(spot(1, width + 1), height, activate(jnp.where(even, a, b)), wide)
            for row in range(height):
                store(spot(row + 1, 1), width, activate(x_ref[f, row]))
            for row in range(tall):
                for dx in range(3):
                    for t, (lane, size) in enumerate(lane_tiles):
                        value = grid[t, pl.ds(spot(row, dx), width), 0:size].astype(BF16)
                        to = dx * main + lane if lane < main else 3 * main + dx * tail + lane - main
                        act[at, row, :, to : to + size] = value

        def tap(dy, low, high):
            above = taps[dy - 1, :, :, low:high] if dy else first_taps[:, :, low:high]
            below = tails[dy - 1, :, :, low:high] if dy else first_tails[:, :, low:high]
            parts = [above.reshape(3 * main, high - low), below.reshape(deep, high - low)]
            return jnp.concatenate(parts, axis=0)

        def row_taps(part, dy):
            act = acts[part]
            lhs = act[:, dy : dy + height].reshape(per_part * height * width, act.shape[3])
            return jnp.dot(lhs, tap(dy, 0, main), preferred_element_type=F32)

        def side_of(part):
            act = acts[part]
            lhs = act[...].reshape(per_part * tall * width, act.shape[3])
            side = jnp.dot(lhs, side_taps[...], preferred_element_type=F32)
            side = side.reshape(per_part, tall, width, 3 * tail)
            return sum(side[:, dy : dy + height, :, dy * tail : (dy + 1) * tail] for dy in range(3))

        def finish(part, total, side):
            total = total.reshape(per_part, height, width, main)
            bias = bias_ref[...].reshape(1, 1, channels)
            for at in range(per_part):
                f = part * per_part + at
                for values, low, high in ((total, 0, main), (side, main, channels)):
                    value = values[at] + bias[:, :, low:high]
                    if last:
                        value = value + skip_ref[f, :, :, low:high].astype(F32)
                    else:
                        value = value + extra_ref[f : f + 1, low:high].reshape(1, 1, high - low)
                    staged_ref[f, :, :, low:high] = value.astype(BF16)
                if not last:
                    put_edges(f, staged_ref[f], sides_ref, ends_ref)
                    pairs.append(frame_stats(staged_ref, f))
            if last:
                span = pl.ds(part * per_part, per_part)
                pltpu.make_async_copy(staged_ref.at[span], out_ref.at[span], out_sem.at[part]).start()

        pairs = []
        for part in range(PARTS):
            for f in range(part * per_part, (part + 1) * per_part):
                prepare(f)
            sums[part][...] = row_taps(part, 0)
        side_taps[:, 0:tail] = tap(0, main, channels)
        for dy in (1, 2):
            for copy in copies[2 * dy - 2 : 2 * dy]:
                copy.wait()
            side_taps[:, dy * tail : (dy + 1) * tail] = tap(dy, main, channels)
            if dy == 1:
                if not last:
                    for copy in next_copies:
                        copy.start()
                for part in range(PARTS):
                    sums[part][...] += row_taps(part, 1)
        if last:
            skip_copy.wait()
        for part in range(PARTS):
            finish(part, sums[part][...] + row_taps(part, 2), side_of(part))
        if last:
            for part in range(PARTS):
                span = pl.ds(part * per_part, per_part)
                pltpu.make_async_copy(staged_ref.at[span], out_ref.at[span], out_sem.at[part]).wait()
        else:
            write_stats(pairs, float(height * width), own_stats_ref)
            for copy in next_copies:
                copy.wait()


def edge_shapes(x):
    frames, height, width, channels = x.shape
    return [
        jax.ShapeDtypeStruct((2, frames, height, channels), BF16),
        jax.ShapeDtypeStruct((2, frames, width, channels), BF16),
    ]


def stats_shape(x, devices):
    return jax.ShapeDtypeStruct((devices, 2, x.shape[0] * GROUPS), F32)


def tap_shapes(channels):
    main = (channels // DEEP) * DEEP
    tail = channels - main
    slots = -(-3 * tail // DEEP) * DEEP // tail
    return (3, main, channels), (slots, tail, channels)


def call_edges(x, weight, devices):
    taps, tails = tap_shapes(x.shape[3])
    out_shape = [jax.ShapeDtypeStruct(x.shape, x.dtype), *edge_shapes(x), stats_shape(x, devices)]
    out_shape += [jax.ShapeDtypeStruct(taps, BF16), jax.ShapeDtypeStruct(tails, BF16)]
    return pl.pallas_call(
        edges_kernel,
        out_shape=out_shape,
        in_specs=[HBM, HBM],
        out_specs=[VMEM] * len(out_shape),
        scratch_shapes=[pltpu.SemaphoreType.DMA((x.shape[0],)), pltpu.SemaphoreType.DMA((2,))],
        name="edges",
        compiler_params=pltpu.CompilerParams(vmem_limit_bytes=12 << 20),
    )(in_hbm(x), in_hbm(weight))


def call_conv(x, halo, stats, gain, shift, bias, first, weight, extra, following, devices):
    frames, height, width, channels = x.shape
    main = (channels // DEEP) * DEEP
    tail = channels - main
    taps, tails = tap_shapes(channels)
    depth = 3 * main + tails[0] * tail
    last = following is None
    part = frames // PARTS
    cells = -(-part * (height + 2) * (width + 2) // 8) * 8
    scratch = [
        pltpu.VMEM((2, *taps), BF16),
        pltpu.VMEM((2, *tails), BF16),
        pltpu.VMEM((depth, 3 * tail), BF16),
        pltpu.SemaphoreType.DMA((2, 2)),
    ]
    scratch += [pltpu.VMEM((-(-channels // LANES), cells, LANES), F32)] * PARTS
    scratch += [pltpu.VMEM((part, height + 2, width, depth), BF16)] * PARTS
    scratch += [pltpu.VMEM((part * height * width, main), F32)] * PARTS
    out_shape = [jax.ShapeDtypeStruct(x.shape, BF16)]
    if last:
        out_specs = [HBM]
        operands, specs = [in_hbm(extra)], [HBM]
        scratch = [
            pltpu.VMEM(x.shape, BF16), pltpu.SemaphoreType.DMA((1,)),
            pltpu.VMEM(x.shape, BF16), pltpu.SemaphoreType.DMA((PARTS,)),
        ] + scratch
    else:
        out_shape += [*edge_shapes(x), stats_shape(x, devices)]
        out_shape += [jax.ShapeDtypeStruct(taps, BF16), jax.ShapeDtypeStruct(tails, BF16)]
        out_specs = [VMEM] * len(out_shape)
        operands, specs = [extra, in_hbm(following)], [VMEM, HBM]
        scratch = [pltpu.SemaphoreType.DMA((2,))] + scratch
    out = pl.pallas_call(
        functools.partial(conv_kernel, last),
        out_shape=out_shape,
        in_specs=[VMEM] * 11 + [HBM] + specs,
        out_specs=out_specs,
        scratch_shapes=scratch,
        name="second_conv" if last else "first_conv",
        compiler_params=pltpu.CompilerParams(vmem_limit_bytes=24 << 20),
    )(x, *halo, stats, gain, shift, bias, *first, in_hbm(weight), *operands)
    return out[0] if last else out


def halo_of(sides, ends):
    columns, rows = lax.axis_size("lon"), lax.axis_size("lat")
    half = columns // 2
    down, even = place()
    paired = [(k, k ^ 1) for k in range(columns)]
    crossed = [(k, (k + 1) % columns if k % 2 else (k - 1) % columns) for k in range(columns)]
    clockwise = []
    for k in range(columns):
        for r in range(rows):
            if k < half:
                to = (k, r + 1) if r < rows - 1 else (k + half, r)
            else:
                to = (k, r - 1) if r > 0 else (k - half, r)
            clockwise.append((k * rows + r, to[0] * rows + to[1]))
    counter = [(b, a) for a, b in clockwise]
    a = lax.ppermute(sides[0], "lon", paired)
    b = lax.ppermute(sides[1], "lon", crossed)

    def whole_row(end, here):
        a_end = jnp.where(here, a[:, -1], a[:, 0])[:, None]
        b_end = jnp.where(here, b[:, -1], b[:, 0])[:, None]
        west, east = jnp.where(even, b_end, a_end), jnp.where(even, a_end, b_end)
        return jnp.concatenate([west, end, east], axis=1)

    cw = lax.ppermute(whole_row(ends[0], down), AXES, clockwise)
    ccw = lax.ppermute(whole_row(ends[1], ~down), AXES, counter)
    return a, b, cw, ccw


def share(own):
    return lax.all_to_all(own, AXES, 0, 0)


def on_device(
    latent, norm1_gain, norm1_shift, conv1_weight, conv1_bias, emb_shift,
    norm2_gain, norm2_shift, conv2_weight, conv2_bias,
):
    devices = lax.axis_size("lon") * lax.axis_size("lat")
    held, sides, ends, own, *first = call_edges(latent, conv1_weight, devices)
    halo = halo_of(sides, ends)
    hidden, sides, ends, own, *first = call_conv(
        held, halo, share(own), norm1_gain, norm1_shift, conv1_bias, first, conv1_weight,
        emb_shift, conv2_weight, devices)
    halo = halo_of(sides, ends)
    return call_conv(
        hidden, halo, share(own), norm2_gain, norm2_shift, conv2_bias, first, conv2_weight,
        latent, None, devices)


def solution(mesh):
    placed = (P(None, "lat", "lon", None), P(), P(), P(), P(), P(), P(), P(), P(), P())
    return jax.shard_map(
        on_device,
        mesh=mesh,
        in_specs=placed,
        out_specs=P(None, "lat", "lon", None),
        check_vma=False,
    )
```

time: 50.4 us -> 53.4 us (1.060)
  local copies, waits for them, and re-layouts: 0.08 us -> 6.26 us
  Pallas kernels: 16.2 us -> 13 us
    unnamed x14 -> x20, local copies, waits for them, and re-layouts: 0.03 us -> 6.22 us
    pallas_call x3 -> x1, Pallas kernels: 5.46 us -> 3.42 us  [call_edges(): pl.pallas_call(edges_kernel, out_shape=out_shape, in_specs=[HBM, HBM], ou...]
    pallas_call x2, Pallas kernels: 10.7 us -> 9.54 us  [call_conv(): pl.pallas_call(functools.partial(conv_kernel, last), out_shape=out_shape,...]
where the time goes in v3:
time: 53.4 us; the launch traced here: 53 us
  starting transfers between devices  20.7 us (39%)
  Pallas kernels  13 us (24%)
  waiting for transfers between devices  12.8 us (24%)
  local copies, waits for them, and re-layouts  6.26 us (12%)
    all_to_all x2, starting transfers between devices, share(): return lax.all_to_all(own, AXES, 0, 0)  11.2 us
    pallas_call x2, Pallas kernels, call_conv(): pl.pallas_call(functools.partial(conv_kernel, last), out_shape=out_shape,...  9.54 us
    unnamed x20, local copies, waits for them, and re-layouts  6.22 us
    ppermute x2, starting transfers between devices, halo_of(): b = lax.ppermute(sides[1], 'lon', crossed)  4.91 us
    ppermute x2, waiting for transfers between devices, halo_of(): ccw = lax.ppermute(whole_row(ends[1], ~down), AXES, counter)  4.54 us
    ppermute x2, starting transfers between devices, halo_of(): cw = lax.ppermute(whole_row(ends[0], down), AXES, clockwise)  4.46 us
    ppermute x2, waiting for transfers between devices, halo_of(): b = lax.ppermute(sides[1], 'lon', crossed)  4.1 us
    ppermute x2, waiting for transfers between devices, halo_of(): cw = lax.ppermute(whole_row(ends[0], down), AXES, clockwise)  3.49 us
  transfers between devices with their start and end apart: 10, of which 8 were waited for; matrix products, arithmetic and copies ran while one was open for 1% of the time, Pallas kernels for 0%

profile of v3, /device:TPU:0, one launch (start us, length us, event | category | flops | bytes accessed | tf_op | source)
XLA Modules:
  0.0 53.0 jit_solution(14038611282740630406)
XLA Ops:
  0.0 0.0 copy-start.3
  0.0 3.4 %edges.1 = (bf16[4,16,16,320]{3,2,1,0:T(8,128)(2,1)S(1)}, bf16[2,4,16,320]{3,2,1,0:T(8,128)(2,1)S(1)}, bf16[2,4,16,320]{3,2,1,0:T(8,128)(2,1)S(1)}, f32[32,2,128...) custom-call(bf16[4,16,16,320]{3,2,1,0:T(8,128)(2,1)} %extra_ref.3, ...), custom_call_target="tpu_custom_call" | custom-call | tf_op jit(solution)/shard_map/edges/pallas_call | solution.py:316
  3.4 7.3 %all-to-all-start = ((f32[32,2,128]{2,1,0:T(2,128)}), f32[32,2,128]{2,1,0:T(2,128)S(1)}, u32[]{:S(2)}, u32[]{:S(2)}) async-start(f32[32,2,128]{2,1,0:T(2,128)} %get-tuple-element.20), calls=%async_computation | async-start | bytes 65536 | tf_op jit(solution)/shard_map/all_to_all | solution.py:401
  10.8 2.5 %collective-permute-start.1 = (bf16[4,16,320]{2,1,0:T(8,128)(2,1)S(1)}, bf16[4,16,320]{2,1,0:T(8,128)(2,1)S(1)}, u32[]{:S(2)}, u32[]{:S(2)}) collective-permute-start(bf16[4,16,320]{2,1,0:T(8,128)(2,1)S(1)} %get-tuple-element.43), channel_id=1, source_target_pairs={{0,28},{4,8},{8,4},{12,16},{16,12},{20,24},{24,20},{28,0},{1,29},{... | collective-permute-start | bytes 122888 | tf_op jit(solution)/shard_map/ppermute | solution.py:387
  13.2 0.0 collective-permute-start
  13.3 2.0 %collective-permute-done.1.b_ref = bf16[4,16,320]{2,1,0:T(8,128)(2,1)S(1)} collective-permute-done((bf16[4,16,320]{2,1,0:T(8,128)(2,1)S(1)}, bf16[4,16,320]{2,1,0:T(8,128)(2,1)S(1)}, u32[]{:S(2)}, u32[]{:S(2)}) %collective-permute-start.1) | collective-permute-done | bytes 40992 | tf_op jit(solution)/shard_map/ppermute | solution.py:387
  15.3 0.0 collective-permute-done.a_ref
  15.4 2.2 %collective-permute-start.2 = (bf16[4,18,320]{2,1,0:T(8,128)(2,1)S(1)}, bf16[4,18,320]{2,1,0:T(8,128)(2,1)S(1)}, u32[]{:S(2)}, u32[]{:S(2)}) collective-permute-start(bf16[4,18,320]{2,1,0:T(8,128)(2,1)S(1)} %pad_maximum_fusion), channel_id=1, source_target_pairs={{0,1},{1,2},{2,3},{3,19},{4,5},{5,6},{6,7},{7,23},{8,9},{9,10},{10... | collective-permute-start | bytes 138248 | tf_op jit(solution)/shard_map/ppermute | solution.py:395
  17.7 0.1 collective-permute-start.3
  17.7 0.3 all-to-all-done.stats_ref
  18.1 1.7 %collective-permute-done.2.cw_ref = bf16[4,18,320]{2,1,0:T(8,128)(2,1)S(1)} collective-permute-done((bf16[4,18,320]{2,1,0:T(8,128)(2,1)S(1)}, bf16[4,18,320]{2,1,0:T(8,128)(2,1)S(1)}, u32[]{:S(2)}, u32[]{:S(2)}) %collective-permute-start.2) | collective-permute-done | bytes 46112 | tf_op jit(solution)/shard_map/ppermute | solution.py:395
  19.8 2.3 %collective-permute-done.3.ccw_ref = bf16[4,18,320]{2,1,0:T(8,128)(2,1)S(1)} collective-permute-done((bf16[4,18,320]{2,1,0:T(8,128)(2,1)S(1)}, bf16[4,18,320]{2,1,0:T(8,128)(2,1)S(1)}, u32[]{:S(2)}, u32[]{:S(2)}) %collective-permute-start.3) | collective-permute-done | bytes 46112 | tf_op jit(solution)/shard_map/ppermute | solution.py:396
  22.1 0.0 copy-start
  22.1 0.6 %copy-done = bf16[4,18,320]{2,1,0:T(8,128)(2,1)} copy-done((bf16[4,18,320]{2,1,0:T(8,128)(2,1)}, bf16[4,18,320]{2,1,0:T(8,128)(2,1)S(1)}, u32[]{:S(2)}) %copy-start) | copy-done | bytes 46104
  22.7 0.0 copy-done.3
  22.7 0.0 copy-start.1
  22.7 0.9 %copy-done.1 = bf16[4,18,320]{2,1,0:T(8,128)(2,1)S(1)} copy-done((bf16[4,18,320]{2,1,0:T(8,128)(2,1)S(1)}, bf16[4,18,320]{2,1,0:T(8,128)(2,1)}, u32[]{:S(2)}) %copy-start.1) | copy-done | bytes 46104
  23.6 0.0 copy-start.4
  23.6 0.7 %copy-done.4 = f32[320]{0:T(512)S(1)} copy-done((f32[320]{0:T(512)S(1)}, f32[320]{0:T(512)}, u32[]{:S(2)}) %copy-start.4) | copy-done | bytes 1304
  24.3 0.0 copy-start.5
  24.3 0.7 %copy-done.5 = f32[320]{0:T(512)S(1)} copy-done((f32[320]{0:T(512)S(1)}, f32[320]{0:T(512)}, u32[]{:S(2)}) %copy-start.5) | copy-done | bytes 1304
  25.0 0.0 copy-start.6
  25.0 0.7 %copy-done.6 = f32[320]{0:T(512)S(1)} copy-done((f32[320]{0:T(512)S(1)}, f32[320]{0:T(512)}, u32[]{:S(2)}) %copy-start.6) | copy-done | bytes 1304
  25.6 4.9 %first_conv.1 = (bf16[4,16,16,320]{3,2,1,0:T(8,128)(2,1)S(1)}, bf16[2,4,16,320]{3,2,1,0:T(8,128)(2,1)S(1)}, bf16[2,4,16,320]{3,2,1,0:T(8,128)(2,1)S(1)}, f32[32,...) custom-call(bf16[4,16,16,320]{3,2,1,0:T(8,128)(2,1)S(1)} %get-tuple-element.17.x_ref, ...), custom_call_target="tpu_custom_call" | custom-call | tf_op jit(solution)/shard_map/first_conv/pallas_call | solution.py:359
  30.6 0.0 copy-start.2
  30.6 0.6 %copy-done.2 = f32[32,2,128]{2,1,0:T(2,128)} copy-done((f32[32,2,128]{2,1,0:T(2,128)}, f32[32,2,128]{2,1,0:T(2,128)S(1)}, u32[]{:S(2)}) %copy-start.2) | copy-done | bytes 32792
  31.2 3.8 %all-to-all-start.1 = ((f32[32,2,128]{2,1,0:T(2,128)}), f32[32,2,128]{2,1,0:T(2,128)S(1)}, u32[]{:S(2)}, u32[]{:S(2)}) async-start(f32[32,2,128]{2,1,0:T(2,128)} %copy-done.2), calls=%async_computation.1 | async-start | bytes 65536 | tf_op jit(solution)/shard_map/all_to_all | solution.py:401
  35.1 2.5 %collective-permute-start.5 = (bf16[4,16,320]{2,1,0:T(8,128)(2,1)S(1)}, bf16[4,16,320]{2,1,0:T(8,128)(2,1)S(1)}, u32[]{:S(2)}, u32[]{:S(2)}) collective-permute-start(bf16[4,16,320]{2,1,0:T(8,128)(2,1)S(1)} %get-tuple-element.35), channel_id=1, source_target_pairs={{0,28},{4,8},{8,4},{12,16},{16,12},{20,24},{24,20},{28,0},{1,29},{... | collective-permute-start | bytes 122888 | tf_op jit(solution)/shard_map/ppermute | solution.py:387
  37.5 0.0 collective-permute-start.4
  37.6 2.1 %collective-permute-done.5.b_ref = bf16[4,16,320]{2,1,0:T(8,128)(2,1)S(1)} collective-permute-done((bf16[4,16,320]{2,1,0:T(8,128)(2,1)S(1)}, bf16[4,16,320]{2,1,0:T(8,128)(2,1)S(1)}, u32[]{:S(2)}, u32[]{:S(2)}) %collective-permute-start.5) | collective-permute-done | bytes 40992 | tf_op jit(solution)/shard_map/ppermute | solution.py:387
  39.6 0.0 collective-permute-done.4.a_ref
  39.7 2.2 %collective-permute-start.6 = (bf16[4,18,320]{2,1,0:T(8,128)(2,1)S(1)}, bf16[4,18,320]{2,1,0:T(8,128)(2,1)S(1)}, u32[]{:S(2)}, u32[]{:S(2)}) collective-permute-start(bf16[4,18,320]{2,1,0:T(8,128)(2,1)S(1)} %pad_maximum_fusion.2), channel_id=1, source_target_pairs={{0,1},{1,2},{2,3},{3,19},{4,5},{5,6},{6,7},{7,23},{8,9},{9,10},{10... | collective-permute-start | bytes 138248 | tf_op jit(solution)/shard_map/ppermute | solution.py:395
  42.0 0.1 collective-permute-start.7
  42.0 0.3 all-to-all-done.1.stats_ref
  42.4 1.7 %collective-permute-done.6.cw_ref = bf16[4,18,320]{2,1,0:T(8,128)(2,1)S(1)} collective-permute-done((bf16[4,18,320]{2,1,0:T(8,128)(2,1)S(1)}, bf16[4,18,320]{2,1,0:T(8,128)(2,1)S(1)}, u32[]{:S(2)}, u32[]{:S(2)}) %collective-permute-start.6) | collective-permute-done | bytes 46112 | tf_op jit(solution)/shard_map/ppermute | solution.py:395
  44.1 2.3 %collective-permute-done.7.ccw_ref = bf16[4,18,320]{2,1,0:T(8,128)(2,1)S(1)} collective-permute-done((bf16[4,18,320]{2,1,0:T(8,128)(2,1)S(1)}, bf16[4,18,320]{2,1,0:T(8,128)(2,1)S(1)}, u32[]{:S(2)}, u32[]{:S(2)}) %collective-permute-start.7) | collective-permute-done | bytes 46112 | tf_op jit(solution)/shard_map/ppermute | solution.py:396
  46.4 0.0 copy-start.7
  46.4 0.7 %copy-done.7 = f32[320]{0:T(512)S(1)} copy-done((f32[320]{0:T(512)S(1)}, f32[320]{0:T(512)}, u32[]{:S(2)}) %copy-start.7) | copy-done | bytes 1304
  47.1 0.0 copy-start.8
  47.1 0.7 %copy-done.8 = f32[320]{0:T(512)S(1)} copy-done((f32[320]{0:T(512)S(1)}, f32[320]{0:T(512)}, u32[]{:S(2)}) %copy-start.8) | copy-done | bytes 1304
  47.7 0.0 copy-start.9
  47.7 0.7 %copy-done.9 = f32[320]{0:T(512)S(1)} copy-done((f32[320]{0:T(512)S(1)}, f32[320]{0:T(512)}, u32[]{:S(2)}) %copy-start.9) | copy-done | bytes 1304
  48.4 4.6 %second_conv.1 = bf16[4,16,16,320]{3,2,1,0:T(8,128)(2,1)} custom-call(bf16[4,16,16,320]{3,2,1,0:T(8,128)(2,1)S(1)} %get-tuple-element.23.x_ref, bf16[4,16,320]{2,1,0:T(8,128)(2,1)S(1)} %collective-permute-done.4.a_ref, bf16[4,16,320]{2,1,0:T(8,128)(2,1)S(1)} %collective-permute-done.5.b_ref, bf16[4,18,320]{2,1,0:T(8,128)(2,1)S(1)} %collective-permute-done.6.cw_ref, ...), custom_call_target="tpu_custom_call" | custom-call | tf_op jit(solution)/shard_map/second_conv/pallas_call | solution.py:359
  (10 shorter events, 0.3 us)
Async XLA Ops:
  0.0 22.7 %copy-start.3 = (f32[4,320]{1,0:T(4,128)S(1)}, f32[4,320]{1,0:T(4,128)}, u32[]{:S(2)}) copy-start(f32[4,320]{1,0:T(4,128)} %extra_ref.2) | copy-start | bytes 15364
  3.4 14.6 %all-to-all-start = ((f32[32,2,128]{2,1,0:T(2,128)}), f32[32,2,128]{2,1,0:T(2,128)S(1)}, u32[]{:S(2)}, u32[]{:S(2)}) async-start(f32[32,2,128]{2,1,0:T(2,128)} %get-tuple-element.20), calls=%async_computation | async-start | bytes 65536 | tf_op jit(solution)/shard_map/all_to_all | solution.py:401
  10.8 4.5 %collective-permute-start.1 = (bf16[4,16,320]{2,1,0:T(8,128)(2,1)S(1)}, bf16[4,16,320]{2,1,0:T(8,128)(2,1)S(1)}, u32[]{:S(2)}, u32[]{:S(2)}) collective-permute-start(bf16[4,16,320]{2,1,0:T(8,128)(2,1)S(1)} %get-tuple-element.43), channel_id=1, source_target_pairs={{0,28},{4,8},{8,4},{12,16},{16,12},{20,24},{24,20},{28,0},{1,29},{... | collective-permute-start | bytes 122888 | tf_op jit(solution)/shard_map/ppermute | solution.py:387
  13.2 2.1 %collective-permute-start = (bf16[4,16,320]{2,1,0:T(8,128)(2,1)S(1)}, bf16[4,16,320]{2,1,0:T(8,128)(2,1)S(1)}, u32[]{:S(2)}, u32[]{:S(2)}) collective-permute-start(bf16[4,16,320]{2,1,0:T(8,128)(2,1)S(1)} %get-tuple-element.44), channel_id=1, source_target_pairs={{0,4},{4,0},{8,12},{12,8},{16,20},{20,16},{24,28},{28,24},{1,5},{5... | collective-permute-start | bytes 122888 | tf_op jit(solution)/shard_map/ppermute | solution.py:386
  15.4 4.4 %collective-permute-start.2 = (bf16[4,18,320]{2,1,0:T(8,128)(2,1)S(1)}, bf16[4,18,320]{2,1,0:T(8,128)(2,1)S(1)}, u32[]{:S(2)}, u32[]{:S(2)}) collective-permute-start(bf16[4,18,320]{2,1,0:T(8,128)(2,1)S(1)} %pad_maximum_fusion), channel_id=1, source_target_pairs={{0,1},{1,2},{2,3},{3,19},{4,5},{5,6},{6,7},{7,23},{8,9},{9,10},{10... | collective-permute-start | bytes 138248 | tf_op jit(solution)/shard_map/ppermute | solution.py:395
  17.7 4.4 %collective-permute-start.3 = (bf16[4,18,320]{2,1,0:T(8,128)(2,1)S(1)}, bf16[4,18,320]{2,1,0:T(8,128)(2,1)S(1)}, u32[]{:S(2)}, u32[]{:S(2)}) collective-permute-start(bf16[4,18,320]{2,1,0:T(8,128)(2,1)S(1)} %pad_maximum_fusion.1), channel_id=1, source_target_pairs={{1,0},{2,1},{3,2},{19,3},{5,4},{6,5},{7,6},{23,7},{9,8},{10,9},{11... | collective-permute-start | bytes 138248 | tf_op jit(solution)/shard_map/ppermute | solution.py:396
  22.1 0.6 %copy-start = (bf16[4,18,320]{2,1,0:T(8,128)(2,1)}, bf16[4,18,320]{2,1,0:T(8,128)(2,1)S(1)}, u32[]{:S(2)}) copy-start(bf16[4,18,320]{2,1,0:T(8,128)(2,1)S(1)} %collective-permute-done.3.ccw_ref) | copy-start | bytes 138244
  22.7 0.9 %copy-start.1 = (bf16[4,18,320]{2,1,0:T(8,128)(2,1)S(1)}, bf16[4,18,320]{2,1,0:T(8,128)(2,1)}, u32[]{:S(2)}) copy-start(bf16[4,18,320]{2,1,0:T(8,128)(2,1)} %copy-done) | copy-start | bytes 138244
  23.6 0.7 %copy-start.4 = (f32[320]{0:T(512)S(1)}, f32[320]{0:T(512)}, u32[]{:S(2)}) copy-start(f32[320]{0:T(512)} %gain_ref.2) | copy-start | bytes 3844
  24.3 0.7 %copy-start.5 = (f32[320]{0:T(512)S(1)}, f32[320]{0:T(512)}, u32[]{:S(2)}) copy-start(f32[320]{0:T(512)} %shift_ref.2) | copy-start | bytes 3844
  25.0 0.7 %copy-start.6 = (f32[320]{0:T(512)S(1)}, f32[320]{0:T(512)}, u32[]{:S(2)}) copy-start(f32[320]{0:T(512)} %bias_ref.2) | copy-start | bytes 3844
  30.6 0.6 %copy-start.2 = (f32[32,2,128]{2,1,0:T(2,128)}, f32[32,2,128]{2,1,0:T(2,128)S(1)}, u32[]{:S(2)}) copy-start(f32[32,2,128]{2,1,0:T(2,128)S(1)} %get-tuple-element.26) | copy-start | bytes 98308
  31.2 11.1 %all-to-all-start.1 = ((f32[32,2,128]{2,1,0:T(2,128)}), f32[32,2,128]{2,1,0:T(2,128)S(1)}, u32[]{:S(2)}, u32[]{:S(2)}) async-start(f32[32,2,128]{2,1,0:T(2,128)} %copy-done.2), calls=%async_computation.1 | async-start | bytes 65536 | tf_op jit(solution)/shard_map/all_to_all | solution.py:401
  35.1 4.5 %collective-permute-start.5 = (bf16[4,16,320]{2,1,0:T(8,128)(2,1)S(1)}, bf16[4,16,320]{2,1,0:T(8,128)(2,1)S(1)}, u32[]{:S(2)}, u32[]{:S(2)}) collective-permute-start(bf16[4,16,320]{2,1,0:T(8,128)(2,1)S(1)} %get-tuple-element.35), channel_id=1, source_target_pairs={{0,28},{4,8},{8,4},{12,16},{16,12},{20,24},{24,20},{28,0},{1,29},{... | collective-permute-start | bytes 122888 | tf_op jit(solution)/shard_map/ppermute | solution.py:387
  37.5 2.1 %collective-permute-start.4 = (bf16[4,16,320]{2,1,0:T(8,128)(2,1)S(1)}, bf16[4,16,320]{2,1,0:T(8,128)(2,1)S(1)}, u32[]{:S(2)}, u32[]{:S(2)}) collective-permute-start(bf16[4,16,320]{2,1,0:T(8,128)(2,1)S(1)} %get-tuple-element.36), channel_id=1, source_target_pairs={{0,4},{4,0},{8,12},{12,8},{16,20},{20,16},{24,28},{28,24},{1,5},{5... | collective-permute-start | bytes 122888 | tf_op jit(solution)/shard_map/ppermute | solution.py:386
  39.7 4.4 %collective-permute-start.6 = (bf16[4,18,320]{2,1,0:T(8,128)(2,1)S(1)}, bf16[4,18,320]{2,1,0:T(8,128)(2,1)S(1)}, u32[]{:S(2)}, u32[]{:S(2)}) collective-permute-start(bf16[4,18,320]{2,1,0:T(8,128)(2,1)S(1)} %pad_maximum_fusion.2), channel_id=1, source_target_pairs={{0,1},{1,2},{2,3},{3,19},{4,5},{5,6},{6,7},{7,23},{8,9},{9,10},{10... | collective-permute-start | bytes 138248 | tf_op jit(solution)/shard_map/ppermute | solution.py:395
  42.0 4.4 %collective-permute-start.7 = (bf16[4,18,320]{2,1,0:T(8,128)(2,1)S(1)}, bf16[4,18,320]{2,1,0:T(8,128)(2,1)S(1)}, u32[]{:S(2)}, u32[]{:S(2)}) collective-permute-start(bf16[4,18,320]{2,1,0:T(8,128)(2,1)S(1)} %pad_maximum_fusion.3), channel_id=1, source_target_pairs={{1,0},{2,1},{3,2},{19,3},{5,4},{6,5},{7,6},{23,7},{9,8},{10,9},{11... | collective-permute-start | bytes 138248 | tf_op jit(solution)/shard_map/ppermute | solution.py:396
  46.4 0.7 %copy-start.7 = (f32[320]{0:T(512)S(1)}, f32[320]{0:T(512)}, u32[]{:S(2)}) copy-start(f32[320]{0:T(512)} %gain_ref.3) | copy-start | bytes 3844
  47.1 0.7 %copy-start.8 = (f32[320]{0:T(512)S(1)}, f32[320]{0:T(512)}, u32[]{:S(2)}) copy-start(f32[320]{0:T(512)} %shift_ref.3) | copy-start | bytes 3844
  47.7 0.7 %copy-start.9 = (f32[320]{0:T(512)S(1)}, f32[320]{0:T(512)}, u32[]{:S(2)}) copy-start(f32[320]{0:T(512)} %bias_ref.3) | copy-start | bytes 3844
